TPU v7x, 32 devices: a whole 2x2x4 slice. The times are simulated.
32 devices in a mesh: seq: 8 (over z, y), head: 4 (over x, core).
Axes of the slice: x: 2, y: 2, z: 4, core: 2. Of those that a mesh axis runs over, the one named last changes fastest.
Arguments:
- queries: bfloat16 [8192, 1024], P('seq', 'head'), may hold values from -6 to 6
- keys_values: bfloat16 [8192, 128], P('seq'), may hold values from -6 to 6
- init_state: float32 [64, 2080], replicated, may hold values from -48 to 48
- out_grad: bfloat16 [8192, 1024], P('seq', 'head'), may hold values from -6 to 6
Outputs:
- attended: bfloat16 [8192, 1024], P('seq', 'head')
- query_grad: bfloat16 [8192, 1024], P('seq', 'head')
- kv_grad: float32 [8192, 128], P('seq')
- init_grad: float32 [64, 2080], P(None, 'head')
All inputs are finite; a program needn't handle non-finite values.
Results may differ from a plain program's by a relative error of at most 0.0071.
Values sent between devices are 32-bit elements; how exact they have to be, the bound alone decides.
A program may use at most 128 MiB of HBM per device.

v0:
```python
import jax
import jax.numpy as jnp
import numpy as np
from jax import lax
from jax.sharding import PartitionSpec as P

HEAD_DIM = 64
FEATURES = 2080
GROUP = 1024


epsilon = 1e-06


def entering(part, axis, combine, identity):
    place = lax.axis_index(axis)
    gathered = lax.all_gather(part, axis)
    state = jnp.zeros_like(part) + jnp.asarray(identity, part.dtype)

    def one(step, state):
        return combine(state, lax.dynamic_index_in_dim(gathered, step, 0, False))

    return lax.fori_loop(0, place, one, state)


def pair_tables(width):
    left_index, right_index = np.triu_indices(width)
    factor = np.where(left_index == right_index, 1.0, np.sqrt(2.0)) / np.sqrt(width)
    rows_of = np.arange(width)[:, None]
    left_pick = (rows_of == left_index[None, :]).astype(np.float32)
    right_pick = (rows_of == right_index[None, :]).astype(np.float32)
    return (jnp.asarray(left_pick), jnp.asarray(right_pick), jnp.asarray(factor, jnp.float32))


def product(first, second, contract):
    return lax.dot_general(
        first.astype(jnp.float32),
        second.astype(jnp.float32),
        (contract, ((), ())),
        preferred_element_type=jnp.float32,
    )


def exact_product(first, second, contract):
    return lax.dot_general(
        first,
        second,
        (contract, ((), ())),
        precision=lax.Precision.HIGHEST,
        preferred_element_type=jnp.float32,
    )


def features(wide, tables):
    left_pick, right_pick, factor = tables
    return (
        exact_product(wide, left_pick, ((1,), (0,)))
        * exact_product(wide, right_pick, ((1,), (0,)))
        * factor
    )


def feature_grad(rows_in, upstream, tables):
    left_pick, right_pick, factor = tables
    inner = rows_in.astype(jnp.float32)
    scaled = lax.optimization_barrier(upstream).astype(jnp.float32) * factor
    left_vals = exact_product(inner, left_pick, ((1,), (0,)))
    right_vals = exact_product(inner, right_pick, ((1,), (0,)))
    return exact_product(scaled * right_vals, left_pick, ((1,), (1,))) + exact_product(
        scaled * left_vals, right_pick, ((1,), (1,))
    )


def head_pass(query, keys, values, start_low, grad, tables):
    width = query.shape[1]
    length = query.shape[0]
    qfeat = features(query.astype(jnp.float32), tables).astype(jnp.bfloat16)
    inter = product(qfeat, start_low, ((1,), (1,)))
    logits = product(query, keys, ((1,), (1,)))
    causal = lax.broadcasted_iota(jnp.int32, (length, length), 0) >= lax.broadcasted_iota(
        jnp.int32, (length, length), 1
    )
    weights = jnp.where(causal, logits * logits / width, 0.0).astype(jnp.bfloat16)
    numer = inter + product(weights, values, ((1,), (0,)))
    scale = lax.rsqrt(jnp.mean(numer * numer, axis=1, keepdims=True) + epsilon)
    normed = numer * scale
    upstream = grad.astype(jnp.float32)
    d_numer = (
        scale * (upstream - normed * jnp.mean(upstream * normed, axis=1, keepdims=True))
    ).astype(jnp.bfloat16)
    d_qfeat = product(d_numer, start_low, ((1,), (0,))).astype(jnp.bfloat16)
    d_weights = product(d_numer, values, ((1,), (1,)))
    d_logits = jnp.where(causal, d_weights * logits * (2.0 / width), 0.0).astype(jnp.bfloat16)
    query_total = feature_grad(query, d_qfeat, tables) + product(d_logits, keys, ((1,), (0,)))
    key_local = product(d_logits, query, ((0,), (0,)))
    value_local = product(weights, d_numer, ((0,), (0,)))
    state_local = product(d_numer, qfeat, ((0,), (0,)))
    return (
        normed.astype(jnp.bfloat16),
        query_total.astype(jnp.bfloat16),
        key_local,
        value_local,
        state_local,
    )


def add_states(earlier, later):
    return earlier + later


def per_device(queries, keys_values, init_state, out_grad):
    tables = pair_tables(HEAD_DIM)
    rows = queries.shape[0]
    heads_here = queries.shape[1] // HEAD_DIM
    blocks = rows // GROUP
    slice_width = FEATURES // lax.axis_size("head")
    offset = lax.axis_index("head") * slice_width
    seq_pos = lax.axis_index("seq")
    keys = keys_values[:, :HEAD_DIM]
    values = keys_values[:, HEAD_DIM:]
    key_blocks = keys.reshape(blocks, GROUP, HEAD_DIM)
    value_blocks = values.reshape(blocks, GROUP, HEAD_DIM)
    kfeat = features(keys.astype(jnp.float32), tables).astype(jnp.bfloat16)
    kfeat_blocks = kfeat.reshape(blocks, GROUP, FEATURES)
    updates = lax.map(
        lambda pair: product(pair[0], pair[1], ((0,), (0,))), (value_blocks, kfeat_blocks)
    )
    local_total = jnp.sum(updates, axis=0)
    local_before = jnp.concatenate(
        [jnp.zeros_like(updates), jnp.cumsum(updates[:-1], axis=0)], axis=0
    )
    carried = entering(local_total, "seq", add_states, jnp.zeros_like(local_total))
    starts = (init_state[None] + carried[None] + local_before).astype(jnp.bfloat16)
    query_blocks = queries.reshape(blocks, GROUP, heads_here, HEAD_DIM).transpose(0, 2, 1, 3)
    grad_blocks = out_grad.reshape(blocks, GROUP, heads_here, HEAD_DIM).transpose(0, 2, 1, 3)

    def block_pass(inputs):
        query_heads, key_block, value_block, grad_heads, start_low = inputs

        def one_head(pair):
            return head_pass(pair[0], key_block, value_block, start_low, pair[1], tables)

        normed, qgrad, key_part, value_part, state_part = lax.map(
            one_head, (query_heads, grad_heads)
        )
        return (
            normed,
            qgrad,
            jnp.sum(key_part, axis=0),
            jnp.sum(value_part, axis=0),
            jnp.sum(state_part, axis=0),
        )

    normed_all, qgrad_all, key_local, value_local, state_sum = lax.map(
        block_pass, (query_blocks, key_blocks, value_blocks, grad_blocks, starts)
    )
    attended = normed_all.transpose(0, 2, 1, 3).reshape(rows, heads_here * HEAD_DIM)
    query_grad = qgrad_all.transpose(0, 2, 1, 3).reshape(rows, heads_here * HEAD_DIM)
    grads_here = lax.psum_scatter(state_sum, "head", scatter_dimension=2, tiled=True)
    device_total = jnp.sum(grads_here, axis=0)
    zero_slice = jnp.zeros_like(device_total)
    piece = lax.all_gather(device_total[None], "seq", axis=0, tiled=True)
    order = jnp.arange(piece.shape[0], dtype=jnp.int32)
    keep = (order > seq_pos).astype(jnp.float32)
    after = zero_slice + jnp.sum(piece * keep[:, None, None], axis=0)
    init_grad = zero_slice + jnp.sum(piece, axis=0)
    inclusive = jnp.cumsum(grads_here[::-1], axis=0)[::-1]
    later_local = jnp.concatenate([inclusive[1:], jnp.zeros_like(inclusive[:1])], axis=0)
    later_low = (after[None] + later_local).astype(jnp.bfloat16)
    kslice = lax.dynamic_slice_in_dim(kfeat, offset, slice_width, 1).reshape(
        blocks, GROUP, slice_width
    )

    def key_block_pass(inputs):
        kslice_block, value_block, later_block = inputs
        value_state = product(kslice_block, later_block, ((1,), (1,)))
        d_kslice = product(value_block, later_block, ((1,), (0,))).astype(jnp.bfloat16)
        return (value_state, d_kslice)

    value_state, d_kslice = lax.map(key_block_pass, (kslice, value_blocks, later_low))
    left_pick, right_pick, factor = tables
    slice_tables = (
        lax.dynamic_slice_in_dim(left_pick, offset, slice_width, 1),
        lax.dynamic_slice_in_dim(right_pick, offset, slice_width, 1),
        lax.dynamic_slice_in_dim(factor, offset, slice_width, 0),
    )
    key_state = feature_grad(keys, d_kslice.reshape(rows, slice_width), slice_tables)
    partial_grad = jnp.concatenate(
        [
            key_local.reshape(rows, HEAD_DIM) + key_state,
            (value_local + value_state).reshape(rows, HEAD_DIM),
        ],
        axis=1,
    )
    kv_total = lax.psum(partial_grad, "head")
    return (attended, query_grad, kv_total, init_grad)


def solution(mesh):
    return jax.shard_map(
        per_device,
        mesh=mesh,
        in_specs=(P("seq", "head"), P("seq", None), P(), P("seq", "head")),
        out_specs=(P("seq", "head"), P("seq", "head"), P("seq", None), P(None, "head")),
        check_vma=False,
    )
```

profile of v0, /device:TPU:0, one launch (start us, length us, event | category | flops | bytes accessed | tf_op | source)
XLA Modules:
  0.0 386.8 jit_solution(1485889664631984479)
XLA Ops:
  7.2 4.8 %fusion.66 = f32[2080,1024]{1,0:T(8,128)S(1)} fusion(f32[64,2080]{1,0:T(8,128)} %constant.114.clone, bf16[1024,128]{1,0:T(8,128)(2,1)} %param.12), kind=kOutput, calls=%fused_computation.94 | convolution fusion | flops 1635778560 | bytes 9314304 | tf_op jit(solution)/shard_map/dot_general | solution.py:45
  12.1 5.6 %multiply_convert_fusion.2 = bf16[2080,1024]{1,0:T(8,128)(2,1)S(1)} fusion(f32[2080,1024]{1,0:T(8,128)S(1)} %fusion.66, f32[64,2080]{1,0:T(8,128)S(1)} %copy-done.1, f32[2080]{0:T(1024)S(1)} %copy-done.7, bf16[1024,128]{1,0:T(8,128)(2,1)S(1)} %copy-done.3), kind=kOutput, calls=%fused_computation.56 | convolution fusion | flops 1642168320 | bytes 13582464 | tf_op jit(solution)/shard_map/dot_general | solution.py:45
  17.7 2.0 copy-done.2
  19.7 2.2 convolution_bitcast_fusion.3
  22.3 1.0 copy.22
  23.4 77.4 %all-gather.6.cloned.1.call-done = f32[512,2080]{1,0:T(8,128)} async-done(((f32[64,2080]{1,0:T(8,128)}), f32[512,2080]{1,0:T(8,128)}) %all-gather.6.cloned.1.call-update) | async-done | bytes 4259856 | tf_op jit(solution)/shard_map/all_gather | solution.py:17
  101.0 1.2 add_convert_fusion
  102.2 146.0 %while.33 = (s32[]{:T(128)}, bf16[4,1024,64]{1,2,0:T(8,128)(2,1)}, bf16[4,1024,64]{1,2,0:T(8,128)(2,1)}, f32[4,1024,64]{1,2,0:T(8,128)}, f32[4,1024,64]{1,2,0:T(...) while((s32[]{:T(128)}, bf16[4,1024,64]{1,2,0:T(8,128)(2,1)}, ...), condition=%wide.region_5.6_spmd.clone, body=%wide.region_2.5_spmd.sunk.clone.sunk | while | flops 8204518400 | bytes 102170048 | solution.py:143
  118.7 3.5 fusion.153
  122.2 4.4 %multiply_convert_fusion.4 = (bf16[1024,2080]{0,1:T(8,128)(2,1)S(1)}, f32[1024,2080]{0,1:T(8,128)S(1)}) fusion(f32[1024,2080]{0,1:T(8,128)S(1)} %fusion.153, f32[2080]{0:T(1024)S(1)} %get-tuple-element.458, f32[64,2080]{1,0:T(8,128)S(1)} %get-tuple-element.459, bf16[4,1024,64]{1,2,0:T(8,128)(2,1)S(1)} %get-tuple-element.451, s32[]{:T(128)} %get-tuple-element.430), kind=kOutput, calls=%fused_computation.6.clone.1 | convolution fusion | flops 1642168320 | bytes 21999620 | tf_op jit(solution)/shard_map/while/body/eval_jaxpr/while/body/eval_jaxpr/dot_general | solution.py:45
  127.9 0.9 multiply_reduce_fusion.3
  129.0 2.3 fusion.162
  132.1 1.3 convolution_convert_fusion.3
  133.5 6.6 %fusion.157 = f32[1024,64]{0,1:T(8,128)S(1)} fusion(f32[64,2080]{1,0:T(8,128)S(1)} %get-tuple-element.457, f32[1024,2080]{0,1:T(8,128)S(1)} %get-tuple-element.393, bf16[1024,2080]{0,1:T(8,128)(2,1)S(1)} %convolution_convert_fusion.3, f32[2080]{0:T(1024)S(1)} %get-tuple-element.458), kind=kOutput, calls=%fused_computation.1.clone.1 | convolution fusion | flops 1642168320 | bytes 13582464 | tf_op jit(solution)/shard_map/while/body/eval_jaxpr/while/body/eval_jaxpr/dot_general | solution.py:45
  140.1 6.6 %fusion.158 = f32[1024,64]{0,1:T(8,128)S(1)} fusion(f32[1024,64]{0,1:T(8,128)S(1)} %fusion.157, f32[64,2080]{1,0:T(8,128)S(1)} %get-tuple-element.459, f32[1024,2080]{0,1:T(8,128)S(1)} %fusion.153, bf16[1024,2080]{0,1:T(8,128)(2,1)S(1)} %convolution_convert_fusion.3, f32[2080]{0:T(1024)S(1)} %get-tuple-element.458), kind=kOutput, calls=%fused_computation.21.clone.1 | convolution fusion | flops 1642233856 | bytes 13844608 | tf_op jit(solution)/shard_map/while/body/eval_jaxpr/while/body/eval_jaxpr/dot_general | solution.py:45
  146.7 1.4 fusion.159
  148.1 1.2 fusion.160
  149.3 1.1 fusion.161
  151.1 3.5 fusion.153
  154.7 4.4 %multiply_convert_fusion.4 = (bf16[1024,2080]{0,1:T(8,128)(2,1)S(1)}, f32[1024,2080]{0,1:T(8,128)S(1)}) fusion(f32[1024,2080]{0,1:T(8,128)S(1)} %fusion.153, f32[2080]{0:T(1024)S(1)} %get-tuple-element.458, f32[64,2080]{1,0:T(8,128)S(1)} %get-tuple-element.459, bf16[4,1024,64]{1,2,0:T(8,128)(2,1)S(1)} %get-tuple-element.451, s32[]{:T(128)} %get-tuple-element.430), kind=kOutput, calls=%fused_computation.6.clone.1 | convolution fusion | flops 1642168320 | bytes 21999620 | tf_op jit(solution)/shard_map/while/body/eval_jaxpr/while/body/eval_jaxpr/dot_general | solution.py:45
  160.4 0.9 multiply_reduce_fusion.3
  161.5 2.2 fusion.162
  164.5 1.3 convolution_convert_fusion.3
  165.8 6.6 %fusion.157 = f32[1024,64]{0,1:T(8,128)S(1)} fusion(f32[64,2080]{1,0:T(8,128)S(1)} %get-tuple-element.457, f32[1024,2080]{0,1:T(8,128)S(1)} %get-tuple-element.393, bf16[1024,2080]{0,1:T(8,128)(2,1)S(1)} %convolution_convert_fusion.3, f32[2080]{0:T(1024)S(1)} %get-tuple-element.458), kind=kOutput, calls=%fused_computation.1.clone.1 | convolution fusion | flops 1642168320 | bytes 13582464 | tf_op jit(solution)/shard_map/while/body/eval_jaxpr/while/body/eval_jaxpr/dot_general | solution.py:45
  172.4 6.6 %fusion.158 = f32[1024,64]{0,1:T(8,128)S(1)} fusion(f32[1024,64]{0,1:T(8,128)S(1)} %fusion.157, f32[64,2080]{1,0:T(8,128)S(1)} %get-tuple-element.459, f32[1024,2080]{0,1:T(8,128)S(1)} %fusion.153, bf16[1024,2080]{0,1:T(8,128)(2,1)S(1)} %convolution_convert_fusion.3, f32[2080]{0:T(1024)S(1)} %get-tuple-element.458), kind=kOutput, calls=%fused_computation.21.clone.1 | convolution fusion | flops 1642233856 | bytes 13844608 | tf_op jit(solution)/shard_map/while/body/eval_jaxpr/while/body/eval_jaxpr/dot_general | solution.py:45
  179.1 1.4 fusion.159
  180.5 1.2 fusion.160
  181.7 1.1 fusion.161
  183.5 3.5 fusion.153
  187.0 4.4 %multiply_convert_fusion.4 = (bf16[1024,2080]{0,1:T(8,128)(2,1)S(1)}, f32[1024,2080]{0,1:T(8,128)S(1)}) fusion(f32[1024,2080]{0,1:T(8,128)S(1)} %fusion.153, f32[2080]{0:T(1024)S(1)} %get-tuple-element.458, f32[64,2080]{1,0:T(8,128)S(1)} %get-tuple-element.459, bf16[4,1024,64]{1,2,0:T(8,128)(2,1)S(1)} %get-tuple-element.451, s32[]{:T(128)} %get-tuple-element.430), kind=kOutput, calls=%fused_computation.6.clone.1 | convolution fusion | flops 1642168320 | bytes 21999620 | tf_op jit(solution)/shard_map/while/body/eval_jaxpr/while/body/eval_jaxpr/dot_general | solution.py:45
  192.7 0.9 multiply_reduce_fusion.3
  193.8 2.2 fusion.162
  196.8 1.3 convolution_convert_fusion.3
  198.2 6.6 %fusion.157 = f32[1024,64]{0,1:T(8,128)S(1)} fusion(f32[64,2080]{1,0:T(8,128)S(1)} %get-tuple-element.457, f32[1024,2080]{0,1:T(8,128)S(1)} %get-tuple-element.393, bf16[1024,2080]{0,1:T(8,128)(2,1)S(1)} %convolution_convert_fusion.3, f32[2080]{0:T(1024)S(1)} %get-tuple-element.458), kind=kOutput, calls=%fused_computation.1.clone.1 | convolution fusion | flops 1642168320 | bytes 13582464 | tf_op jit(solution)/shard_map/while/body/eval_jaxpr/while/body/eval_jaxpr/dot_general | solution.py:45
  204.8 6.6 %fusion.158 = f32[1024,64]{0,1:T(8,128)S(1)} fusion(f32[1024,64]{0,1:T(8,128)S(1)} %fusion.157, f32[64,2080]{1,0:T(8,128)S(1)} %get-tuple-element.459, f32[1024,2080]{0,1:T(8,128)S(1)} %fusion.153, bf16[1024,2080]{0,1:T(8,128)(2,1)S(1)} %convolution_convert_fusion.3, f32[2080]{0:T(1024)S(1)} %get-tuple-element.458), kind=kOutput, calls=%fused_computation.21.clone.1 | convolution fusion | flops 1642233856 | bytes 13844608 | tf_op jit(solution)/shard_map/while/body/eval_jaxpr/while/body/eval_jaxpr/dot_general | solution.py:45
  211.4 1.4 fusion.159
  212.8 1.2 fusion.160
  214.0 1.1 fusion.161
  215.8 3.5 fusion.153
  219.3 4.4 %multiply_convert_fusion.4 = (bf16[1024,2080]{0,1:T(8,128)(2,1)S(1)}, f32[1024,2080]{0,1:T(8,128)S(1)}) fusion(f32[1024,2080]{0,1:T(8,128)S(1)} %fusion.153, f32[2080]{0:T(1024)S(1)} %get-tuple-element.458, f32[64,2080]{1,0:T(8,128)S(1)} %get-tuple-element.459, bf16[4,1024,64]{1,2,0:T(8,128)(2,1)S(1)} %get-tuple-element.451, s32[]{:T(128)} %get-tuple-element.430), kind=kOutput, calls=%fused_computation.6.clone.1 | convolution fusion | flops 1642168320 | bytes 21999620 | tf_op jit(solution)/shard_map/while/body/eval_jaxpr/while/body/eval_jaxpr/dot_general | solution.py:45
  225.1 0.9 multiply_reduce_fusion.3
  226.1 2.3 fusion.162
  229.2 1.3 convolution_convert_fusion.3
  230.5 6.6 %fusion.157 = f32[1024,64]{0,1:T(8,128)S(1)} fusion(f32[64,2080]{1,0:T(8,128)S(1)} %get-tuple-element.457, f32[1024,2080]{0,1:T(8,128)S(1)} %get-tuple-element.393, bf16[1024,2080]{0,1:T(8,128)(2,1)S(1)} %convolution_convert_fusion.3, f32[2080]{0:T(1024)S(1)} %get-tuple-element.458), kind=kOutput, calls=%fused_computation.1.clone.1 | convolution fusion | flops 1642168320 | bytes 13582464 | tf_op jit(solution)/shard_map/while/body/eval_jaxpr/while/body/eval_jaxpr/dot_general | solution.py:45
  237.1 6.6 %fusion.158 = f32[1024,64]{0,1:T(8,128)S(1)} fusion(f32[1024,64]{0,1:T(8,128)S(1)} %fusion.157, f32[64,2080]{1,0:T(8,128)S(1)} %get-tuple-element.459, f32[1024,2080]{0,1:T(8,128)S(1)} %fusion.153, bf16[1024,2080]{0,1:T(8,128)(2,1)S(1)} %convolution_convert_fusion.3, f32[2080]{0:T(1024)S(1)} %get-tuple-element.458), kind=kOutput, calls=%fused_computation.21.clone.1 | convolution fusion | flops 1642233856 | bytes 13844608 | tf_op jit(solution)/shard_map/while/body/eval_jaxpr/while/body/eval_jaxpr/dot_general | solution.py:45
  243.8 1.4 fusion.159
  245.2 1.2 fusion.160
  246.4 1.1 fusion.161
  248.2 2.6 reduce_sum.75
  252.1 39.2 %all-reduce.6.cloned.1.call-done = f32[1,64,2080]{2,1,0:T(8,128)} async-done(((f32[1,64,2080]{2,1,0:T(8,128)}), f32[1,64,2080]{2,1,0:T(8,128)}) %all-reduce.6.cloned.1.call-update) | async-done | bytes 532496
  291.3 1.7 constant_dynamic-slice_fusion
  293.2 1.2 fusion.48
  294.4 2.6 fusion.52
  297.0 2.0 reduce_sum.74
  299.0 2.0 reduce_sum.77
  301.0 34.9 %all-gather.4.cloned.1.call-done = f32[8,64,520]{2,1,0:T(8,128)} async-done(((f32[1,64,520]{2,1,0:T(8,128)}), f32[8,64,520]{2,1,0:T(8,128)}) %all-gather.4.cloned.1.call-update) | async-done | bytes 1064976 | tf_op jit(solution)/shard_map/all_gather | solution.py:162
  336.0 2.3 fusion.68
  338.9 1.6 convolution_add_fusion.2
  340.5 2.0 fusion.40
  342.6 2.0 fusion.44
  345.5 1.0 copy.24
  346.5 1.0 copy.25
  347.5 30.4 %all-reduce.4.cloned.1.call-done = f32[1024,128]{0,1:T(8,128)} async-done(((f32[1024,128]{0,1:T(8,128)}), f32[1024,128]{0,1:T(8,128)}) %all-reduce.4.cloned.1.call-update) | async-done | bytes 524304 | tf_op jit(solution)/shard_map/psum | solution.py:195
  377.8 2.0 copy.26
  (87 shorter events, 14.4 us)
Async XLA Ops:
  7.2 4.9 %copy-start.1 = (f32[64,2080]{1,0:T(8,128)S(1)}, f32[64,2080]{1,0:T(8,128)}, u32[]{:S(2)}) copy-start(f32[64,2080]{1,0:T(8,128)} %constant.115.clone) | copy-start | bytes 1597444
  7.2 4.9 %copy-start.7 = (f32[2080]{0:T(1024)S(1)}, f32[2080]{0:T(1024)}, u32[]{:S(2)}) copy-start(f32[2080]{0:T(1024)} %constant.116.clone) | copy-start | bytes 24964
  7.2 4.9 %copy-start.3 = (bf16[1024,128]{1,0:T(8,128)(2,1)S(1)}, bf16[1024,128]{1,0:T(8,128)(2,1)}, u32[]{:S(2)}) copy-start(bf16[1024,128]{1,0:T(8,128)(2,1)} %param.12) | copy-start | bytes 786436
  7.2 93.7 %all-gather.6.cloned.1.call-start = ((), (), s32[]{:S(2)}) async-start(), calls=%async_computation.2 | async-start | bytes 5013504 | tf_op jit(solution)/shard_map/all_gather | solution.py:17
  17.6 2.0 copy-start.2
  19.7 2.4 copy-start.9
  19.7 2.6 copy-start.10
  22.0 269.4 %all-reduce.6.cloned.1.call-start = ((), (), s32[]{:S(2)}) async-start(), calls=%async_computation.3 | async-start | bytes 1114112
  100.9 1.2 copy-start
  102.1 148.7 %copy-start.13 = (u32[32]{0:T(128)S(1)}, u32[32]{0:T(128)}, u32[]{:S(2)}) copy-start(u32[32]{0:T(128)} %constant.119) | copy-start | bytes 388
  102.1 191.1 %copy-start.4 = (bf16[1024,128]{1,0:T(8,128)(2,1)S(1)}, bf16[1024,128]{1,0:T(8,128)(2,1)}, u32[]{:S(2)}) copy-start(bf16[1024,128]{1,0:T(8,128)(2,1)} %param.12) | copy-start | bytes 786436
  127.4 1.5 copy-start.6
  159.8 1.5 copy-start.6
  192.1 1.5 copy-start.6
  224.5 1.5 copy-start.6
  250.8 85.1 %all-gather.4.cloned.1.call-start = ((), (), s32[]{:S(2)}) async-start(), calls=%async_computation | async-start | bytes 1474560 | tf_op jit(solution)/shard_map/all_gather | solution.py:162
  293.1 84.8 %all-reduce.4.cloned.1.call-start = ((), (), s32[]{:S(2)}) async-start(), calls=%async_computation.1 | async-start | bytes 1048576 | tf_op jit(solution)/shard_map/psum | solution.py:195
  336.0 6.6 %copy-start.5 = (f32[520,1024]{1,0:T(8,128)S(1)}, f32[520,1024]{1,0:T(8,128)}, u32[]{:S(2)}) copy-start(f32[520,1024]{1,0:T(8,128)} %fusion.52) | copy-start | bytes 6389764
  336.0 6.6 %copy-start.8 = (f32[1024,64]{0,1:T(8,128)S(1)}, f32[1024,64]{0,1:T(8,128)}, u32[]{:S(2)}) copy-start(f32[1024,64]{0,1:T(8,128)} %reduce_sum.74) | copy-start | bytes 786436
  342.5 2.9 copy-start.11
  342.6 3.9 %copy-start.12 = (bf16[4,1024,64]{1,2,0:T(8,128)(2,1)S(1)}, bf16[4,1024,64]{1,2,0:T(8,128)(2,1)}, u32[]{:S(2)}) copy-start(bf16[4,1024,64]{1,2,0:T(8,128)(2,1)} %get-tuple-element.177) | copy-start | bytes 1572868
Sparse Core Ops, SparseCore 0:
  22.1 78.7 all-gather.5
  250.9 40.3 all-reduce.5
  294.1 41.8 all-gather.3
  345.6 32.2 all-reduce.3
where the time goes:
time: 394 us; the launch traced here: 387 us
  waiting for transfers between devices  182 us (46%)
  matrix products  149 us (38%)
  loops' own time  16.9 us (4%)
  between operations  15.1 us (4%)
  other arithmetic  14.2 us (4%)
  local copies, waits for them, and re-layouts  9.91 us (3%)
    dot_general x22, matrix products, exact_product(): lax.dot_general(first, second, (contract, ((), ())), precision=lax.Precis...  103 us
    all_gather x1, waiting for transfers between devices, entering(): gathered = lax.all_gather(part, axis)  77.4 us
    dot_general x39, matrix products, product(): lax.dot_general(first.astype(jnp.float32), second.astype(jnp.float32), (c...  45.7 us
    unnamed x5, waiting for transfers between devices  39.3 us
    all_gather x1, waiting for transfers between devices, per_device(): piece = lax.all_gather(device_total[None], 'seq', axis=0, tiled=True)  34.9 us
    psum x1, waiting for transfers between devices, per_device(): kv_total = lax.psum(partial_grad, 'head')  30.4 us
    another operation x1, loops' own time, block_pass(): lax.map(one_head, (query_heads, grad_heads))  16.9 us
    unnamed x33, local copies, waits for them, and re-layouts  9.64 us
  transfers between devices with their start and end apart: 4, of which 4 were waited for; matrix products, arithmetic and copies ran while one was open for 3% of the time, Pallas kernels for 0%

commit v1 on v0

v1 whole, which is shorter than its diff:
```python
import functools

import jax
import jax.numpy as jnp
import numpy as np
from jax import lax
from jax.experimental import pallas as pl
from jax.experimental.pallas import tpu as pltpu
from jax.sharding import PartitionSpec as P

HEAD_DIM = 64
GROUP = 1024
EPS = 1e-06
CHUNK = 256
MESH = pl.DeviceIdType.MESH
F32, BF16 = jnp.float32, jnp.bfloat16


def padded_layout(width):
    starts, at = [], 0
    for a in range(width):
        starts.append(at)
        at += width - a // 8 * 8
    return starts, at


STARTS, PADDED = padded_layout(HEAD_DIM)
CANON = [a * HEAD_DIM - a * (a - 1) // 2 for a in range(HEAD_DIM)]


def dot(first, second, contract=((1,), (0,))):
    return lax.dot_general(first, second, (contract, ((), ())), preferred_element_type=F32)


def edge_weights(cols):
    row = lax.broadcasted_iota(jnp.int32, (8, cols), 0)
    return [
        jnp.where(row < m, 0.0, jnp.where(row == m, float(np.sqrt(0.5)), 1.0)).astype(F32)
        for m in range(8)
    ]


def write_features(x_ref, xs_ref, f_ref, cols):
    edges = edge_weights(cols)
    for a in range(0, HEAD_DIM, 2):
        base = a // 8 * 8
        parts = []
        for c in (a, a + 1):
            prod = x_ref[c : c + 1, :] * xs_ref[base:, :]
            parts.append(prod[:8] * edges[c % 8])
            if base + 8 < HEAD_DIM:
                parts.append(prod[8:])
        at = STARTS[a]
        f_ref[at : at + 2 * (HEAD_DIM - base), :] = jnp.concatenate(parts, axis=0).astype(BF16)


def feature_grad(xs_ref, df_ref, row_ref, cols):
    edges = edge_weights(cols)
    tiles = HEAD_DIM // 8
    acc = [jnp.zeros((8, cols), F32) for _ in range(tiles)]
    for a in range(HEAD_DIM):
        first = a // 8
        xa = jnp.broadcast_to(xs_ref[a : a + 1, :], (8, cols))
        total = None
        for t in range(first, tiles):
            at = STARTS[a] + (t - first) * 8
            part = df_ref[at : at + 8, :]
            if t == first:
                part = part * edges[a % 8]
            acc[t] = acc[t] + part * xa
            term = part * xs_ref[t * 8 : t * 8 + 8, :]
            total = term if total is None else total + term
        row_ref[a : a + 1, :] = jnp.sum(total, axis=0, keepdims=True)
    return jnp.concatenate(acc, axis=0) + row_ref[...]


def scaled(x):
    return x * float(np.sqrt(2.0 / HEAD_DIM))


def prepare_kernel(rows, init_ref, kv_ref, initp_ref, u_ref, padt, kvt, xs, f):
    h = lax.axis_index("head")
    tokens = kv_ref.shape[0]
    padt[...] = jnp.zeros_like(padt)
    for a in range(HEAD_DIM):
        at = STARTS[a] + a % 8
        padt[at : at + HEAD_DIM - a, :] = init_ref[CANON[a] : CANON[a] + HEAD_DIM - a, :]
    initp_ref[...] = padt[...].T
    kvt[...] = kv_ref[...].astype(F32).T
    vals = kvt[pl.ds(pl.multiple_of(HEAD_DIM + h * rows, 8), rows), :].astype(BF16)
    for c in range(tokens // CHUNK):
        at = slice(c * CHUNK, (c + 1) * CHUNK)
        x = kvt.at[:HEAD_DIM, at]
        xs[...] = scaled(x[...])
        write_features(x, xs, f, CHUNK)
        part = dot(vals[:, at], f[...], ((1,), (1,)))
        if c == 0:
            u_ref[...] = part
        else:
            u_ref[...] += part


def head_kernel(
    q_ref, kv_ref, initp_ref, carry_ref, og_ref,
    att_ref, qg_ref, kvl_ref, sg_ref,
    qt, ogt, attt, qgt, start, startt, keys, vals, kt, vt, f, df, x, xs, row,
):
    tokens = q_ref.shape[0]
    heads = q_ref.shape[1] // HEAD_DIM
    qt[...] = q_ref[...].astype(F32).T
    ogt[...] = og_ref[...].astype(F32).T
    kvt = kv_ref[...].astype(F32).T
    kt[...] = kvt[:HEAD_DIM].astype(BF16)
    vt[...] = kvt[HEAD_DIM:].astype(BF16)
    keys[...] = kv_ref[:, :HEAD_DIM]
    vals[...] = kv_ref[:, HEAD_DIM:]
    first = initp_ref[...] + carry_ref[...]
    start[...] = first.astype(BF16)
    startt[...] = first.T.astype(BF16)
    kvl_ref[...] = jnp.zeros_like(kvl_ref)
    sg_ref[...] = jnp.zeros_like(sg_ref)
    causal = lax.broadcasted_iota(jnp.int32, (CHUNK, CHUNK), 0) <= lax.broadcasted_iota(
        jnp.int32, (CHUNK, CHUNK), 1
    )

    def masked(full):
        n = full.shape[0]
        last = jnp.where(causal, full[n - CHUNK :], 0.0)
        if n == CHUNK:
            return last.astype(BF16)
        return jnp.concatenate([full[: n - CHUNK], last], axis=0).astype(BF16)

    for c in range(tokens // CHUNK):
        n = (c + 1) * CHUNK
        at = slice(c * CHUNK, n)

        def one_head(h, _):
            here = pl.ds(pl.multiple_of(h * HEAD_DIM, HEAD_DIM), HEAD_DIM)
            query = qt[here, at]
            x[...] = query
            xs[...] = scaled(query)
            write_features(x, xs, f, CHUNK)
            low = query.astype(BF16)
            logits = dot(keys[:n], low)
            weights = masked(logits * logits * (1.0 / HEAD_DIM))
            numer = dot(start[...], f[...]) + dot(vt[:, :n], weights)
            scale = lax.rsqrt(jnp.mean(numer * numer, axis=0, keepdims=True) + EPS)
            normed = numer * scale
            up = ogt[here, at]
            attt[here, at] = normed
            dn = (scale * (up - normed * jnp.mean(up * normed, axis=0, keepdims=True))).astype(BF16)
            df[...] = dot(startt[...], dn)
            dw = dot(vals[:n], dn)
            dl = masked(dw * logits * (2.0 / HEAD_DIM))
            qgt[here, at] = dot(kt[:, :n], dl) + feature_grad(xs, df, row, CHUNK)
            kvl_ref[:n, :HEAD_DIM] += dot(dl, low, ((1,), (1,)))
            kvl_ref[:n, HEAD_DIM:] += dot(weights, dn, ((1,), (1,)))
            sg_ref[...] += dot(dn, f[...], ((1,), (1,)))
            return 0

        lax.fori_loop(0, heads, one_head, 0)
    att_ref[...] = attt[...].T.astype(BF16)
    qg_ref[...] = qgt[...].T.astype(BF16)


def peers(ns, nh):
    s, h = lax.axis_index("seq"), lax.axis_index("head")
    groups = ns // 2
    g, p = s // 2, s % 2
    partner = (s + 1 - 2 * p, h)
    ring = [(lax.rem(g + k, groups) * 2 + p, h) for k in range(1, groups)]
    across = [(s, lax.rem(h + k, nh)) for k in range(1, nh)]
    return s, h, g, p, partner, ring, across


def greet(devices):
    barrier = pltpu.get_barrier_semaphore()
    for device in devices:
        pl.semaphore_signal(barrier, inc=1, device_id=device, device_id_type=MESH)
    pl.semaphore_wait(barrier, len(devices))


def remote(src, dst, sends, recvs, k, device):
    return pltpu.make_async_remote_copy(
        src_ref=src, dst_ref=dst, send_sem=sends.at[k], recv_sem=recvs.at[k],
        device_id=device, device_id_type=MESH,
    )


def prefix_kernel(ns, nh, u_ref, out_ref, pair, both, got, pre, ps, pr, rs, rr, hs, hr):
    rows = u_ref.shape[0]
    s, h, g, p, partner, ring, across = peers(ns, nh)
    greet([partner] + ring + across)
    swap = remote(u_ref, pair, ps, pr, 0, partner)
    swap.start()
    swap.wait()
    both[...] = u_ref[...] + pair[...]
    moves = [remote(both, got.at[k], rs, rr, k, ring[k]) for k in range(len(ring))]
    for k, move in enumerate(moves):
        @pl.when(g + k + 1 < ns // 2)
        def _(move=move):
            move.start()
    pre[...] = jnp.where(p == 1, pair[...], 0.0)
    for k, move in enumerate(moves):
        @pl.when(g - k - 1 >= 0)
        def _(move=move, k=k):
            move.wait_recv()
            pre[...] += got[k]
    here = out_ref.at[pl.ds(pl.multiple_of(h * rows, 8), rows), :]
    spread = [remote(pre, here, hs, hr, k, across[k]) for k in range(len(across))]
    for copy in spread:
        copy.start()
    here[...] = pre[...]
    for k, move in enumerate(moves):
        @pl.when(g + k + 1 < ns // 2)
        def _(move=move):
            move.wait_send()
    for copy in spread:
        copy.wait()


def suffix_kernel(
    ns, nh, sg_ref, kvl_ref, later_ref, total_ref, kvq_ref,
    parts, kvparts, own, pair, both, got, late, tot,
    ss, sr, ks, kr, ps, pr, rs, rr, hs, hr, ts, tr,
):
    rows = sg_ref.shape[0] // nh
    quarter = kvl_ref.shape[0] // nh
    s, h, g, p, partner, ring, across = peers(ns, nh)
    greet([partner] + ring + across)
    scatter, kvscatter = [], []
    for k in range(nh - 1):
        to = lax.rem(h + k + 1, nh)
        src = sg_ref.at[pl.ds(pl.multiple_of(to * rows, 8), rows), :]
        scatter.append(remote(src, parts.at[k], ss, sr, k, across[k]))
    for copy in scatter:
        copy.start()
    for k in range(nh - 1):
        to = lax.rem(h + k + 1, nh)
        src = kvl_ref.at[pl.ds(pl.multiple_of(to * quarter, 8), quarter), :]
        kvscatter.append(remote(src, kvparts.at[k], ks, kr, k, across[k]))
    own[...] = sg_ref[pl.ds(pl.multiple_of(h * rows, 8), rows), :]
    for k, copy in enumerate(scatter):
        copy.wait()
        own[...] += parts[k]
    swap = remote(own, pair, ps, pr, 0, partner)
    swap.start()
    for copy in kvscatter:
        copy.start()
    swap.wait()
    both[...] = own[...] + pair[...]
    moves = [remote(both, got.at[k], rs, rr, k, ring[k]) for k in range(len(ring))]
    for move in moves:
        move.start()
    kvsum = kvl_ref[pl.ds(pl.multiple_of(h * quarter, 8), quarter), :]
    for k, copy in enumerate(kvscatter):
        copy.wait()
        kvsum = kvsum + kvparts[k]
    kvq_ref[...] = kvsum
    late[...] = jnp.where(p == 0, pair[...], 0.0)
    tot[...] = both[...]
    for k, move in enumerate(moves):
        move.wait_recv()
        tot[...] += got[k]
        late[...] += jnp.where(k + 1 > g, got[k], 0.0)
    at = pl.ds(pl.multiple_of(h * rows, 8), rows)
    spread = [remote(late, later_ref.at[at, :], hs, hr, k, across[k]) for k in range(nh - 1)]
    spread += [remote(tot, total_ref.at[at, :], ts, tr, k, across[k]) for k in range(nh - 1)]
    for copy in spread:
        copy.start()
    later_ref[at, :] = late[...]
    total_ref[at, :] = tot[...]
    for move in moves:
        move.wait_send()
    for copy in spread:
        copy.wait()


def key_kernel(kv_ref, later_ref, kvq_ref, out_ref, kvt, low, lowt, f, df, xs, row, gt):
    h = lax.axis_index("head")
    quarter = kvq_ref.shape[0]
    block = kv_ref[pl.ds(pl.multiple_of(h * quarter, 16), quarter), :]
    kvt[...] = block.astype(F32).T
    low[...] = later_ref[...].astype(BF16)
    lowt[...] = later_ref[...].T.astype(BF16)
    x = kvt.at[:HEAD_DIM, :]
    xs[...] = scaled(x[...])
    write_features(x, xs, f, quarter)
    gt[HEAD_DIM:, :] = dot(low[...], f[...])
    df[...] = dot(lowt[...], kvt[HEAD_DIM:, :].astype(BF16))
    gt[:HEAD_DIM, :] = feature_grad(xs, df, row, quarter)
    out_ref[...] = kvq_ref[...] + gt[...].T


def finish_kernel(ns, nh, part_ref, total_ref, kv_ref, init_ref, padt, canon, hs, hr):
    quarter = part_ref.shape[0]
    s, h, g, p, partner, ring, across = peers(ns, nh)
    greet(across)
    here = kv_ref.at[pl.ds(pl.multiple_of(h * quarter, 8), quarter), :]
    spread = [remote(part_ref, here, hs, hr, k, across[k]) for k in range(nh - 1)]
    for copy in spread:
        copy.start()
    here[...] = part_ref[...]
    padt[...] = total_ref[...].T
    for a in range(HEAD_DIM):
        at = STARTS[a] + a % 8
        canon[CANON[a] : CANON[a] + HEAD_DIM - a, :] = padt[at : at + HEAD_DIM - a, :]
    wide = init_ref.shape[0]
    init_ref[...] = canon[pl.ds(pl.multiple_of(h * wide, 8), wide), :]
    for copy in spread:
        copy.wait()


def call(kernel, outs, scratch, ins, collective=None):
    params = dict(vmem_limit_bytes=60 * 1024 * 1024)
    if collective is not None:
        params.update(collective_id=collective, has_side_effects=True)
    vmem = pl.BlockSpec(memory_space=pltpu.VMEM)
    return pl.pallas_call(
        kernel,
        out_shape=tuple(jax.ShapeDtypeStruct(shape, dtype) for shape, dtype in outs),
        in_specs=[vmem] * len(ins),
        out_specs=tuple(vmem for _ in outs),
        scratch_shapes=scratch,
        compiler_params=pltpu.CompilerParams(**params),
    )(*ins)


def per_device(ns, nh, queries, keys_values, init_state, out_grad):
    tokens, wide = queries.shape
    assert tokens == GROUP and ns % 2 == 0
    features = init_state.shape[1]
    rows, quarter = HEAD_DIM // nh, tokens // nh
    groups = ns // 2
    V, D = pltpu.VMEM, pltpu.SemaphoreType.DMA

    initp, u = call(
        functools.partial(prepare_kernel, rows),
        [((HEAD_DIM, PADDED), F32), ((rows, PADDED), F32)],
        [V((PADDED, HEAD_DIM), F32), V((2 * HEAD_DIM, tokens), F32),
         V((HEAD_DIM, CHUNK), F32), V((PADDED, CHUNK), BF16)],
        (init_state.T, keys_values),
    )
    part = (rows, PADDED)
    (carry,) = call(
        functools.partial(prefix_kernel, ns, nh),
        [((HEAD_DIM, PADDED), F32)],
        [V(part, F32), V(part, F32), V((groups - 1,) + part, F32), V(part, F32),
         D((1,)), D((1,)), D((groups - 1,)), D((groups - 1,)), D((nh - 1,)), D((nh - 1,))],
        (u,), 1,
    )
    attended, query_grad, kvl, sg = call(
        head_kernel,
        [((tokens, wide), BF16), ((tokens, wide), BF16),
         ((tokens, 2 * HEAD_DIM), F32), ((HEAD_DIM, PADDED), F32)],
        [V((wide, tokens), F32)] * 4
        + [V((HEAD_DIM, PADDED), BF16), V((PADDED, HEAD_DIM), BF16)]
        + [V((tokens, HEAD_DIM), BF16)] * 2 + [V((HEAD_DIM, tokens), BF16)] * 2
        + [V((PADDED, CHUNK), BF16), V((PADDED, CHUNK), F32)]
        + [V((HEAD_DIM, CHUNK), F32)] * 3,
        (queries, keys_values, initp, carry, out_grad),
    )
    later, total, kvq = call(
        functools.partial(suffix_kernel, ns, nh),
        [((HEAD_DIM, PADDED), F32), ((HEAD_DIM, PADDED), F32), ((quarter, 2 * HEAD_DIM), F32)],
        [V((nh - 1,) + part, F32), V((nh - 1, quarter, 2 * HEAD_DIM), F32),
         V(part, F32), V(part, F32), V(part, F32), V((groups - 1,) + part, F32),
         V(part, F32), V(part, F32)]
        + [D((nh - 1,))] * 4 + [D((1,))] * 2 + [D((groups - 1,))] * 2 + [D((nh - 1,))] * 4,
        (sg, kvl), 2,
    )
    (mine,) = call(
        key_kernel,
        [((quarter, 2 * HEAD_DIM), F32)],
        [V((2 * HEAD_DIM, quarter), F32), V((HEAD_DIM, PADDED), BF16),
         V((PADDED, HEAD_DIM), BF16), V((PADDED, quarter), BF16), V((PADDED, quarter), F32),
         V((HEAD_DIM, quarter), F32), V((HEAD_DIM, quarter), F32), V((2 * HEAD_DIM, quarter), F32)],
        (keys_values, later, kvq),
    )
    kv_grad, init_grad = call(
        functools.partial(finish_kernel, ns, nh),
        [((tokens, 2 * HEAD_DIM), F32), ((features // nh, HEAD_DIM), F32)],
        [V((PADDED, HEAD_DIM), F32), V((features, HEAD_DIM), F32), D((nh - 1,)), D((nh - 1,))],
        (mine, total), 3,
    )
    return (attended, query_grad, kv_grad, init_grad.T)


def solution(mesh):
    ns, nh = mesh.shape["seq"], mesh.shape["head"]
    return jax.shard_map(
        functools.partial(per_device, ns, nh),
        mesh=mesh,
        in_specs=(P("seq", "head"), P("seq", None), P(), P("seq", "head")),
        out_specs=(P("seq", "head"), P("seq", "head"), P("seq", None), P(None, "head")),
        check_vma=False,
    )
```

time: 394 us -> 133 us (0.34)
  the two profiles are of different devices: /device:TPU:0 before, /device:TPU:9 now
where the time goes in v1:
time: 133 us
  Pallas kernels  126 us (95%)
  local copies, waits for them, and re-layouts  6.01 us (5%)
    pallas_call x6, Pallas kernels, call(): pl.pallas_call(kernel, out_shape=tuple((jax.ShapeDtypeStruct(shape, dtype...  126 us
    unnamed x3, local copies, waits for them, and re-layouts  6.01 us

profile of v1, /device:TPU:9, one launch (start us, length us, event | category | flops | bytes accessed | tf_op | source)
XLA Modules:
  0.0 133.1 jit_solution(7707603299165295696)
XLA Ops:
  0.6 2.4 %copy.8 = f32[64,2080]{0,1:T(8,128)} copy(f32[64,2080]{1,0:T(8,128)} %param.6) | data formatting | bytes 1064960 | tf_op args[2]
  3.0 3.6 %shard_map.75 = (f32[64,2304]{1,0:T(8,128)}, f32[16,2304]{1,0:T(8,128)}) custom-call(f32[2080,64]{1,0:T(8,128)} %bitcast.2, bf16[1024,128]{1,0:T(8,128)(2,1)} %kv_ref.5), custom_call_target="tpu_custom_call" | custom-call | tf_op jit(solution)/shard_map/pallas_call | solution.py:319
  6.6 21.9 %shard_map.76.carry_ref = f32[64,2304]{1,0:T(8,128)} custom-call(f32[16,2304]{1,0:T(8,128)} %get-tuple-element.16.u_ref), custom_call_target="tpu_custom_call" | custom-call | tf_op jit(solution)/shard_map/pallas_call | solution.py:319
  28.6 35.9 %shard_map.77 = (bf16[1024,256]{1,0:T(8,128)(2,1)}, bf16[1024,256]{1,0:T(8,128)(2,1)}, f32[1024,128]{1,0:T(8,128)}, f32[64,2304]{1,0:T(8,128)}) custom-call(bf16[1024,256]{1,0:T(8,128)(2,1)} %q_ref.1, bf16[1024,128]{1,0:T(8,128)(2,1)} %kv_ref.5, f32[64,2304]{1,0:T(8,128)} %get-tuple-element.15.initp_ref, f32[64,2304]{1,0:T(8,128)} %shard_map.76.carry_ref, ...), custom_call_target="tpu_custom_call" | custom-call | tf_op jit(solution)/shard_map/pallas_call | solution.py:319
  64.4 52.0 %shard_map.78 = (f32[64,2304]{1,0:T(8,128)}, f32[64,2304]{1,0:T(8,128)}, f32[256,128]{1,0:T(8,128)}) custom-call(f32[64,2304]{1,0:T(8,128)} %get-tuple-element.19.sg_ref, f32[1024,128]{1,0:T(8,128)} %get-tuple-element.20.kvl_ref), custom_call_target="tpu_custom_call" | custom-call | tf_op jit(solution)/shard_map/pallas_call | solution.py:319
  116.5 2.8 %shard_map.79.part_ref = f32[256,128]{1,0:T(8,128)} custom-call(bf16[1024,128]{1,0:T(8,128)(2,1)} %kv_ref.5, f32[64,2304]{1,0:T(8,128)} %get-tuple-element.21.later_ref, f32[256,128]{1,0:T(8,128)} %get-tuple-element.22.kvq_ref), custom_call_target="tpu_custom_call" | custom-call | tf_op jit(solution)/shard_map/pallas_call | solution.py:319
  119.3 10.1 %shard_map.80 = (f32[1024,128]{1,0:T(8,128)}, f32[520,64]{1,0:T(8,128)}) custom-call(f32[256,128]{1,0:T(8,128)} %shard_map.79.part_ref, f32[64,2304]{1,0:T(8,128)} %get-tuple-element.23.total_ref), custom_call_target="tpu_custom_call" | custom-call | tf_op jit(solution)/shard_map/pallas_call | solution.py:319
  129.5 1.8 %copy.9 = f32[64,520]{1,0:T(8,128)} copy(f32[64,520]{0,1:T(8,128)} %bitcast.3) | data formatting | bytes 266240
  131.2 1.9 %copy.11 = f32[1024,128]{1,0:T(8,128)} copy(f32[1024,128]{1,0:T(8,128)} %get-tuple-element.36) | data formatting | bytes 1048576

commit v2 on v1

--- a/solution.py
+++ b/solution.py
@@ -78,13 +78,17 @@
     return x * float(np.sqrt(2.0 / HEAD_DIM))
 
 
-def prepare_kernel(rows, init_ref, kv_ref, initp_ref, u_ref, padt, kvt, xs, f):
+def prepare_kernel(rows, init_ref, kv_ref, initp_ref, u_ref, wide, tall, padt, kvt, xs, f):
     h = lax.axis_index("head")
     tokens = kv_ref.shape[0]
+    features = init_ref.shape[1]
     padt[...] = jnp.zeros_like(padt)
+    wide[:, features // 128 * 128 :] = jnp.zeros_like(wide[:, features // 128 * 128 :])
+    wide[:, :features] = init_ref[...]
+    tall[...] = wide[...].T
     for a in range(HEAD_DIM):
         at = STARTS[a] + a % 8
-        padt[at : at + HEAD_DIM - a, :] = init_ref[CANON[a] : CANON[a] + HEAD_DIM - a, :]
+        padt[at : at + HEAD_DIM - a, :] = tall[CANON[a] : CANON[a] + HEAD_DIM - a, :]
     initp_ref[...] = padt[...].T
     kvt[...] = kv_ref[...].astype(F32).T
     vals = kvt[pl.ds(pl.multiple_of(HEAD_DIM + h * rows, 8), rows), :].astype(BF16)
@@ -163,14 +167,15 @@
     qg_ref[...] = qgt[...].T.astype(BF16)
 
 
-def peers(ns, nh):
+def places(ns, nh):
     s, h = lax.axis_index("seq"), lax.axis_index("head")
     groups = ns // 2
     g, p = s // 2, s % 2
+    beside = h + 1 - 2 * (h % 2)
     partner = (s + 1 - 2 * p, h)
     ring = [(lax.rem(g + k, groups) * 2 + p, h) for k in range(1, groups)]
     across = [(s, lax.rem(h + k, nh)) for k in range(1, nh)]
-    return s, h, g, p, partner, ring, across
+    return s, h, g, p, beside, partner, ring, across
 
 
 def greet(devices):
@@ -180,107 +185,191 @@
     pl.semaphore_wait(barrier, len(devices))
 
 
-def remote(src, dst, sends, recvs, k, device):
-    return pltpu.make_async_remote_copy(
-        src_ref=src, dst_ref=dst, send_sem=sends.at[k], recv_sem=recvs.at[k],
-        device_id=device, device_id_type=MESH,
-    )
-
-
-def prefix_kernel(ns, nh, u_ref, out_ref, pair, both, got, pre, ps, pr, rs, rr, hs, hr):
-    rows = u_ref.shape[0]
-    s, h, g, p, partner, ring, across = peers(ns, nh)
+def block(index, size):
+    return pl.ds(pl.multiple_of(index * size, 8), size)
+
+
+class Links:
+    def __init__(self, sends, recvs):
+        self.sends, self.recvs, self.used = sends, recvs, 0
+
+    def copy(self, src, dst, device):
+        k = self.used
+        self.used += 1
+        return pltpu.make_async_remote_copy(
+            src_ref=src, dst_ref=dst, send_sem=self.sends.at[k], recv_sem=self.recvs.at[k],
+            device_id=device, device_id_type=MESH,
+        )
+
+
+def gather_copies(links, nh, s, h, beside, src, out, size, spot):
+    far = []
+    for k in range(2, nh, 2):
+        to = lax.rem(h + k, nh)
+        first = links.copy(src, out.at[spot(h)], (s, to))
+        came = out.at[spot(lax.rem(h + nh - k, nh))]
+        far.append((first, links.copy(came, came, (s, beside))))
+    near = links.copy(src, out.at[spot(h)], (s, beside))
+    return far, near
+
+
+def spread_piece(links, nh, s, h, beside, out, half, slot):
+    spot = lambda owner: block(owner * 2 + slot, half)
+    return gather_copies(links, nh, s, h, beside, out.at[spot(h)], out, half, spot)
+
+
+def start_gather(gather):
+    far, near = gather
+    for first, _ in far:
+        first.start()
+    near.start()
+
+
+def forward_gather(gather):
+    for first, second in gather[0]:
+        first.wait_recv()
+        second.start()
+
+
+def finish_gather(gather):
+    far, near = gather
+    for first, second in far:
+        first.wait_send()
+        second.wait()
+    near.wait()
+
+
+def prefix_kernel(ns, nh, u_ref, out_ref, pair, both, got, mate, sends, recvs):
+    half = u_ref.shape[0] // 2
+    groups = ns // 2
+    s, h, g, p, beside, partner, ring, across = places(ns, nh)
+    links = Links(sends, recvs)
     greet([partner] + ring + across)
-    swap = remote(u_ref, pair, ps, pr, 0, partner)
+    swap = links.copy(u_ref.at[block(1 - p, half), :], pair, partner)
     swap.start()
     swap.wait()
-    both[...] = u_ref[...] + pair[...]
-    moves = [remote(both, got.at[k], rs, rr, k, ring[k]) for k in range(len(ring))]
+    mine = u_ref[block(p, half), :]
+    both[...] = mine + pair[...]
+    moves = [links.copy(both, got.at[k], ring[k]) for k in range(groups - 1)]
     for k, move in enumerate(moves):
-        @pl.when(g + k + 1 < ns // 2)
+        @pl.when(g + k + 1 < groups)
         def _(move=move):
             move.start()
-    pre[...] = jnp.where(p == 1, pair[...], 0.0)
+    ours = block(h * 2 + p, half)
+    theirs = block(h * 2 + 1 - p, half)
+    out_ref[ours, :] = jnp.where(p == 1, pair[...], 0.0)
+    mate[...] = jnp.where(p == 0, mine, 0.0)
     for k, move in enumerate(moves):
         @pl.when(g - k - 1 >= 0)
         def _(move=move, k=k):
             move.wait_recv()
-            pre[...] += got[k]
-    here = out_ref.at[pl.ds(pl.multiple_of(h * rows, 8), rows), :]
-    spread = [remote(pre, here, hs, hr, k, across[k]) for k in range(len(across))]
-    for copy in spread:
-        copy.start()
-    here[...] = pre[...]
+            out_ref[ours, :] += got[k]
+            mate[...] += got[k]
+    back = links.copy(mate, out_ref.at[ours, :], partner)
+    back.start()
+    own_half = spread_piece(links, nh, s, h, beside, out_ref, half, p)
+    start_gather(own_half)
+    other_half = spread_piece(links, nh, s, h, beside, out_ref, half, 1 - p)
+    back.wait_recv()
+    start_gather(other_half)
+    forward_gather(own_half)
+    forward_gather(other_half)
     for k, move in enumerate(moves):
-        @pl.when(g + k + 1 < ns // 2)
+        @pl.when(g + k + 1 < groups)
         def _(move=move):
             move.wait_send()
-    for copy in spread:
-        copy.wait()
+    back.wait_send()
+    finish_gather(own_half)
+    finish_gather(other_half)
 
 
 def suffix_kernel(
     ns, nh, sg_ref, kvl_ref, later_ref, total_ref, kvq_ref,
-    parts, kvparts, own, pair, both, got, late, tot,
-    ss, sr, ks, kr, ps, pr, rs, rr, hs, hr, ts, tr,
+    near, far, mid, kvparts, own, pair, both, got, mate, tot, sends, recvs,
 ):
     rows = sg_ref.shape[0] // nh
+    half = rows // 2
+    groups = ns // 2
     quarter = kvl_ref.shape[0] // nh
-    s, h, g, p, partner, ring, across = peers(ns, nh)
+    s, h, g, p, beside, partner, ring, across = places(ns, nh)
+    links = Links(sends, recvs)
     greet([partner] + ring + across)
-    scatter, kvscatter = [], []
+    evens = range(2, nh + 1, 2)
+    first = []
+    for i, k in enumerate(evens):
+        src = sg_ref.at[block(lax.rem(beside + k, nh), rows), :]
+        first.append(links.copy(src, near.at[i], (s, beside)))
+    for copy in first:
+        copy.start()
+    second = []
+    for i, k in enumerate(evens):
+        first[i].wait_recv()
+        summed = sg_ref[block(lax.rem(h + k, nh), rows), :] + near[i]
+        if k == nh:
+            own[...] = summed
+        else:
+            mid[i] = summed
+            second.append(links.copy(mid.at[i], far.at[i], (s, lax.rem(h + k, nh))))
+            second[-1].start()
+    kvscatter = []
     for k in range(nh - 1):
-        to = lax.rem(h + k + 1, nh)
-        src = sg_ref.at[pl.ds(pl.multiple_of(to * rows, 8), rows), :]
-        scatter.append(remote(src, parts.at[k], ss, sr, k, across[k]))
-    for copy in scatter:
-        copy.start()
-    for k in range(nh - 1):
-        to = lax.rem(h + k + 1, nh)
-        src = kvl_ref.at[pl.ds(pl.multiple_of(to * quarter, 8), quarter), :]
-        kvscatter.append(remote(src, kvparts.at[k], ks, kr, k, across[k]))
-    own[...] = sg_ref[pl.ds(pl.multiple_of(h * rows, 8), rows), :]
-    for k, copy in enumerate(scatter):
-        copy.wait()
-        own[...] += parts[k]
-    swap = remote(own, pair, ps, pr, 0, partner)
+        src = kvl_ref.at[block(lax.rem(h + k + 1, nh), quarter), :]
+        kvscatter.append(links.copy(src, kvparts.at[k], across[k]))
+    for i, copy in enumerate(second):
+        copy.wait_recv()
+        own[...] += far[i]
+    swap = links.copy(own.at[block(1 - p, half), :], pair, partner)
     swap.start()
     for copy in kvscatter:
         copy.start()
     swap.wait()
-    both[...] = own[...] + pair[...]
-    moves = [remote(both, got.at[k], rs, rr, k, ring[k]) for k in range(len(ring))]
+    mine = own[block(p, half), :]
+    both[...] = mine + pair[...]
+    moves = [links.copy(both, got.at[k], ring[k]) for k in range(groups - 1)]
     for move in moves:
         move.start()
-    kvsum = kvl_ref[pl.ds(pl.multiple_of(h * quarter, 8), quarter), :]
+    ours = block(h * 2 + p, half)
+    theirs = block(h * 2 + 1 - p, half)
+    kvsum = kvl_ref[block(h, quarter), :]
     for k, copy in enumerate(kvscatter):
         copy.wait()
         kvsum = kvsum + kvparts[k]
     kvq_ref[...] = kvsum
-    late[...] = jnp.where(p == 0, pair[...], 0.0)
-    tot[...] = both[...]
+    later = jnp.where(p == 0, pair[...], 0.0)
+    mated = jnp.where(p == 1, mine, 0.0)
+    whole = both[...]
     for k, move in enumerate(moves):
         move.wait_recv()
-        tot[...] += got[k]
-        late[...] += jnp.where(k + 1 > g, got[k], 0.0)
-    at = pl.ds(pl.multiple_of(h * rows, 8), rows)
-    spread = [remote(late, later_ref.at[at, :], hs, hr, k, across[k]) for k in range(nh - 1)]
-    spread += [remote(tot, total_ref.at[at, :], ts, tr, k, across[k]) for k in range(nh - 1)]
-    for copy in spread:
-        copy.start()
-    later_ref[at, :] = late[...]
-    total_ref[at, :] = tot[...]
-    for move in moves:
-        move.wait_send()
-    for copy in spread:
-        copy.wait()
+        whole = whole + got[k]
+        after = jnp.where(k + 1 > g, got[k], 0.0)
+        later = later + after
+        mated = mated + after
+    later_ref[ours, :] = later
+    mate[...] = mated
+    tot[...] = whole
+    back = links.copy(mate, later_ref.at[ours, :], partner)
+    back.start()
+    own_half = spread_piece(links, nh, s, h, beside, later_ref, half, p)
+    start_gather(own_half)
+    total_swap = links.copy(tot, total_ref.at[block(p, half), :], partner)
+    total_swap.start()
+    other_half = spread_piece(links, nh, s, h, beside, later_ref, half, 1 - p)
+    back.wait_recv()
+    start_gather(other_half)
+    total_ref[block(p, half), :] = tot[...]
+    forward_gather(own_half)
+    forward_gather(other_half)
+    for copy in first + second + moves + [back]:
+        copy.wait_send()
+    total_swap.wait()
+    finish_gather(own_half)
+    finish_gather(other_half)
 
 
 def key_kernel(kv_ref, later_ref, kvq_ref, out_ref, kvt, low, lowt, f, df, xs, row, gt):
     h = lax.axis_index("head")
     quarter = kvq_ref.shape[0]
-    block = kv_ref[pl.ds(pl.multiple_of(h * quarter, 16), quarter), :]
-    kvt[...] = block.astype(F32).T
+    kvt[...] = kv_ref[pl.ds(pl.multiple_of(h * quarter, 16), quarter), :].astype(F32).T
     low[...] = later_ref[...].astype(BF16)
     lowt[...] = later_ref[...].T.astype(BF16)
     x = kvt.at[:HEAD_DIM, :]
@@ -292,23 +381,58 @@
     out_ref[...] = kvq_ref[...] + gt[...].T
 
 
-def finish_kernel(ns, nh, part_ref, total_ref, kv_ref, init_ref, padt, canon, hs, hr):
+def padded_column(c):
+    a = max(a for a in range(HEAD_DIM) if CANON[a] <= c)
+    return STARTS[a] + a % 8 + c - CANON[a]
+
+
+def windows(features, nh):
+    wide = features // nh
+    ends = [(padded_column(k * wide), padded_column(k * wide + wide - 1)) for k in range(nh)]
+    width = max(-(-(hi + 1) // 128) * 128 - lo // 128 * 128 for lo, hi in ends)
+    return [min(lo // 128 * 128, PADDED - width) for lo, _ in ends], width
+
+
+def window_at(starts, owner, nh):
+    at = starts[0]
+    for k in range(1, nh):
+        at = at + (starts[k] - starts[k - 1]) * ((owner + nh - k) // nh)
+    return at
+
+
+def finish_kernel(
+    ns, nh, starts, width, part_ref, total_ref, kv_ref, init_ref,
+    win, padt, canon, flip, sends, recvs,
+):
     quarter = part_ref.shape[0]
-    s, h, g, p, partner, ring, across = peers(ns, nh)
+    rows = total_ref.shape[0]
+    s, h, g, p, beside, partner, ring, across = places(ns, nh)
+    links = Links(sends, recvs)
     greet(across)
-    here = kv_ref.at[pl.ds(pl.multiple_of(h * quarter, 8), quarter), :]
-    spread = [remote(part_ref, here, hs, hr, k, across[k]) for k in range(nh - 1)]
-    for copy in spread:
-        copy.start()
-    here[...] = part_ref[...]
-    padt[...] = total_ref[...].T
+    spot = lambda owner: block(owner, quarter)
+    parts = gather_copies(links, nh, s, h, beside, part_ref, kv_ref, quarter, spot)
+    start_gather(parts)
+    moves = []
+    for k in range(nh - 1):
+        to = lax.rem(h + k + 1, nh)
+        columns = pl.ds(pl.multiple_of(window_at(starts, to, nh), 128), width)
+        move = links.copy(total_ref.at[:, columns], win.at[block(h, rows), :], across[k])
+        move.start()
+        moves.append(move)
+    mine = pl.ds(pl.multiple_of(window_at(starts, h, nh), 128), width)
+    win[block(h, rows), :] = total_ref[:, mine]
+    kv_ref[spot(h), :] = part_ref[...]
+    forward_gather(parts)
+    for move in moves:
+        move.wait()
+    padt[pl.ds(pl.multiple_of(window_at(starts, h, nh), 128), width), :] = win[...].T
     for a in range(HEAD_DIM):
         at = STARTS[a] + a % 8
         canon[CANON[a] : CANON[a] + HEAD_DIM - a, :] = padt[at : at + HEAD_DIM - a, :]
-    wide = init_ref.shape[0]
-    init_ref[...] = canon[pl.ds(pl.multiple_of(h * wide, 8), wide), :]
-    for copy in spread:
-        copy.wait()
+    wide = init_ref.shape[1]
+    flip[:wide, :] = canon[block(h, wide), :]
+    init_ref[...] = flip[...].T[:, :wide]
+    finish_gather(parts)
 
 
 def call(kernel, outs, scratch, ins, collective=None):
@@ -328,25 +452,29 @@
 
 def per_device(ns, nh, queries, keys_values, init_state, out_grad):
     tokens, wide = queries.shape
-    assert tokens == GROUP and ns % 2 == 0
+    assert tokens == GROUP and ns % 2 == 0 and nh % 2 == 0
     features = init_state.shape[1]
     rows, quarter = HEAD_DIM // nh, tokens // nh
     groups = ns // 2
     V, D = pltpu.VMEM, pltpu.SemaphoreType.DMA
 
+    even = -(-features // 128) * 128
     initp, u = call(
         functools.partial(prepare_kernel, rows),
         [((HEAD_DIM, PADDED), F32), ((rows, PADDED), F32)],
-        [V((PADDED, HEAD_DIM), F32), V((2 * HEAD_DIM, tokens), F32),
+        [V((HEAD_DIM, even), F32), V((even, HEAD_DIM), F32),
+         V((PADDED, HEAD_DIM), F32), V((2 * HEAD_DIM, tokens), F32),
          V((HEAD_DIM, CHUNK), F32), V((PADDED, CHUNK), BF16)],
-        (init_state.T, keys_values),
-    )
-    part = (rows, PADDED)
+        (init_state, keys_values),
+    )
+    part, piece = (rows, PADDED), (rows // 2, PADDED)
+    gathers = nh - 1
+    count = 2 + (groups - 1) + 2 * gathers
     (carry,) = call(
         functools.partial(prefix_kernel, ns, nh),
         [((HEAD_DIM, PADDED), F32)],
-        [V(part, F32), V(part, F32), V((groups - 1,) + part, F32), V(part, F32),
-         D((1,)), D((1,)), D((groups - 1,)), D((groups - 1,)), D((nh - 1,)), D((nh - 1,))],
+        [V(piece, F32), V(piece, F32), V((groups - 1,) + piece, F32), V(piece, F32),
+         D((count,)), D((count,))],
         (u,), 1,
     )
     attended, query_grad, kvl, sg = call(
@@ -360,13 +488,13 @@
         + [V((HEAD_DIM, CHUNK), F32)] * 3,
         (queries, keys_values, initp, carry, out_grad),
     )
+    count = nh // 2 + (nh // 2 - 1) + (nh - 1) + 3 + (groups - 1) + 2 * gathers
     later, total, kvq = call(
         functools.partial(suffix_kernel, ns, nh),
-        [((HEAD_DIM, PADDED), F32), ((HEAD_DIM, PADDED), F32), ((quarter, 2 * HEAD_DIM), F32)],
-        [V((nh - 1,) + part, F32), V((nh - 1, quarter, 2 * HEAD_DIM), F32),
-         V(part, F32), V(part, F32), V(part, F32), V((groups - 1,) + part, F32),
-         V(part, F32), V(part, F32)]
-        + [D((nh - 1,))] * 4 + [D((1,))] * 2 + [D((groups - 1,))] * 2 + [D((nh - 1,))] * 4,
+        [((HEAD_DIM, PADDED), F32), (part, F32), ((quarter, 2 * HEAD_DIM), F32)],
+        [V((nh // 2,) + part, F32)] * 3 + [V((nh - 1, quarter, 2 * HEAD_DIM), F32),
+         V(part, F32), V(piece, F32), V(piece, F32), V((groups - 1,) + piece, F32),
+         V(piece, F32), V(piece, F32), D((count,)), D((count,))],
         (sg, kvl), 2,
     )
     (mine,) = call(
@@ -377,13 +505,17 @@
          V((HEAD_DIM, quarter), F32), V((HEAD_DIM, quarter), F32), V((2 * HEAD_DIM, quarter), F32)],
         (keys_values, later, kvq),
     )
+    starts, width = windows(features, nh)
+    slice_width = features // nh
+    count = gathers + nh - 1
     kv_grad, init_grad = call(
-        functools.partial(finish_kernel, ns, nh),
-        [((tokens, 2 * HEAD_DIM), F32), ((features // nh, HEAD_DIM), F32)],
-        [V((PADDED, HEAD_DIM), F32), V((features, HEAD_DIM), F32), D((nh - 1,)), D((nh - 1,))],
+        functools.partial(finish_kernel, ns, nh, starts, width),
+        [((tokens, 2 * HEAD_DIM), F32), ((HEAD_DIM, slice_width), F32)],
+        [V((HEAD_DIM, width), F32), V((PADDED, HEAD_DIM), F32), V((features, HEAD_DIM), F32),
+         V((-(-slice_width // 128) * 128, HEAD_DIM), F32), D((count,)), D((count,))],
         (mine, total), 3,
     )
-    return (attended, query_grad, kv_grad, init_grad.T)
+    return (attended, query_grad, kv_grad, init_grad)
 
 
 def solution(mesh):

time: 133 us -> 109 us (0.82)
  the two profiles are of different devices: /device:TPU:9 before, /device:TPU:0 now
where the time goes in v2:
time: 109 us
  Pallas kernels  106 us (97%)
  local copies, waits for them, and re-layouts  2.58 us (2%)
    pallas_call x6, Pallas kernels, call(): pl.pallas_call(kernel, out_shape=tuple((jax.ShapeDtypeStruct(shape, dtype...  106 us
    unnamed x4, local copies, waits for them, and re-layouts  2.58 us

profile of v2, /device:TPU:0, one launch (start us, length us, event | category | flops | bytes accessed | tf_op | source)
XLA Modules:
  0.0 109.0 jit_solution(12623459680348921180)
XLA Ops:
  0.6 3.5 %shard_map.75 = (f32[64,2304]{1,0:T(8,128)}, f32[16,2304]{1,0:T(8,128)}) custom-call(f32[64,2080]{1,0:T(8,128)} %init_ref.1, bf16[1024,128]{1,0:T(8,128)(2,1)} %kv_ref.5), custom_call_target="tpu_custom_call" | custom-call | tf_op jit(solution)/shard_map/pallas_call | solution.py:443
  4.2 18.5 %shard_map.76.carry_ref = f32[64,2304]{1,0:T(8,128)} custom-call(f32[16,2304]{1,0:T(8,128)} %get-tuple-element.16.u_ref), custom_call_target="tpu_custom_call" | custom-call | tf_op jit(solution)/shard_map/pallas_call | solution.py:443
  22.7 35.9 %shard_map.77 = (bf16[1024,256]{1,0:T(8,128)(2,1)}, bf16[1024,256]{1,0:T(8,128)(2,1)}, f32[1024,128]{1,0:T(8,128)}, f32[64,2304]{1,0:T(8,128)}) custom-call(bf16[1024,256]{1,0:T(8,128)(2,1)} %q_ref.1, bf16[1024,128]{1,0:T(8,128)(2,1)} %kv_ref.5, f32[64,2304]{1,0:T(8,128)} %get-tuple-element.15.initp_ref, f32[64,2304]{1,0:T(8,128)} %shard_map.76.carry_ref, ...), custom_call_target="tpu_custom_call" | custom-call | tf_op jit(solution)/shard_map/pallas_call | solution.py:443
  58.5 35.0 %shard_map.78 = (f32[64,2304]{1,0:T(8,128)}, f32[16,2304]{1,0:T(8,128)}, f32[256,128]{1,0:T(8,128)}) custom-call(f32[64,2304]{1,0:T(8,128)} %get-tuple-element.19.sg_ref, f32[1024,128]{1,0:T(8,128)} %get-tuple-element.20.kvl_ref), custom_call_target="tpu_custom_call" | custom-call | tf_op jit(solution)/shard_map/pallas_call | solution.py:443
  93.5 2.8 %shard_map.79.part_ref = f32[256,128]{1,0:T(8,128)} custom-call(bf16[1024,128]{1,0:T(8,128)(2,1)} %kv_ref.5, f32[64,2304]{1,0:T(8,128)} %get-tuple-element.21.later_ref, f32[256,128]{1,0:T(8,128)} %get-tuple-element.22.kvq_ref), custom_call_target="tpu_custom_call" | custom-call | tf_op jit(solution)/shard_map/pallas_call | solution.py:443
  96.4 10.0 %shard_map.80 = (f32[1024,128]{1,0:T(8,128)}, f32[64,520]{1,0:T(8,128)}) custom-call(f32[256,128]{1,0:T(8,128)} %shard_map.79.part_ref, f32[16,2304]{1,0:T(8,128)} %get-tuple-element.23.total_ref), custom_call_target="tpu_custom_call" | custom-call | tf_op jit(solution)/shard_map/pallas_call | solution.py:443
  106.4 0.0 copy-start
  106.4 1.9 %copy.10 = f32[1024,128]{1,0:T(8,128)} copy(f32[1024,128]{1,0:T(8,128)} %get-tuple-element.32) | data formatting | bytes 1048576
  108.3 0.0 copy-done
  108.3 0.7 copy.11
Async XLA Ops:
  106.4 1.9 %copy-start = (f32[64,520]{1,0:T(8,128)S(1)}, f32[64,520]{1,0:T(8,128)}, u32[]{:S(2)}) copy-start(f32[64,520]{1,0:T(8,128)} %get-tuple-element.33) | copy-start | bytes 399364

commit v3 on v1

v3 whole, which is shorter than its diff:
```python
import functools

import jax
import jax.numpy as jnp
import numpy as np
from jax import lax
from jax.experimental import pallas as pl
from jax.experimental.pallas import tpu as pltpu
from jax.sharding import PartitionSpec as P

HEAD_DIM = 64
GROUP = 1024
EPS = 1e-06
CHUNK = 256
MESH = pl.DeviceIdType.MESH
F32, BF16 = jnp.float32, jnp.bfloat16


def padded_layout(width):
    starts, at = [], 0
    for a in range(width):
        starts.append(at)
        at += width - a // 8 * 8
    return starts, at


STARTS, PADDED = padded_layout(HEAD_DIM)
CANON = [a * HEAD_DIM - a * (a - 1) // 2 for a in range(HEAD_DIM)]


def dot(first, second, contract=((1,), (0,))):
    return lax.dot_general(first, second, (contract, ((), ())), preferred_element_type=F32)


def edge_weights(cols):
    row = lax.broadcasted_iota(jnp.int32, (8, cols), 0)
    return [
        jnp.where(row < m, 0.0, jnp.where(row == m, float(np.sqrt(0.5)), 1.0)).astype(F32)
        for m in range(8)
    ]


def write_features(x_ref, xs_ref, f_ref, cols):
    edges = edge_weights(cols)
    for a in range(0, HEAD_DIM, 2):
        base = a // 8 * 8
        parts = []
        for c in (a, a + 1):
            prod = x_ref[c : c + 1, :] * xs_ref[base:, :]
            parts.append(prod[:8] * edges[c % 8])
            if base + 8 < HEAD_DIM:
                parts.append(prod[8:])
        at = STARTS[a]
        f_ref[at : at + 2 * (HEAD_DIM - base), :] = jnp.concatenate(parts, axis=0).astype(BF16)


def feature_grad(xs_ref, df_ref, row_ref, cols):
    edges = edge_weights(cols)
    tiles = HEAD_DIM // 8
    acc = [jnp.zeros((8, cols), F32) for _ in range(tiles)]
    for a in range(HEAD_DIM):
        first = a // 8
        xa = jnp.broadcast_to(xs_ref[a : a + 1, :], (8, cols))
        total = None
        for t in range(first, tiles):
            at = STARTS[a] + (t - first) * 8
            part = df_ref[at : at + 8, :]
            if t == first:
                part = part * edges[a % 8]
            acc[t] = acc[t] + part * xa
            term = part * xs_ref[t * 8 : t * 8 + 8, :]
            total = term if total is None else total + term
        row_ref[a : a + 1, :] = jnp.sum(total, axis=0, keepdims=True)
    return jnp.concatenate(acc, axis=0) + row_ref[...]


def scaled(x):
    return x * float(np.sqrt(2.0 / HEAD_DIM))


def places(ns, nh):
    s, h = lax.axis_index("seq"), lax.axis_index("head")
    groups = ns // 2
    g, p = s // 2, s % 2
    beside = h + 1 - 2 * (h % 2)
    partner = (s + 1 - 2 * p, h)
    ring = [(lax.rem(g + k, groups) * 2 + p, h) for k in range(1, groups)]
    across = [(s, lax.rem(h + k, nh)) for k in range(1, nh)]
    return s, h, g, p, beside, partner, ring, across


def block(index, size):
    return pl.ds(pl.multiple_of(index * size, 8), size)


class Links:
    def __init__(self, sends, recvs):
        self.sends, self.recvs, self.used = sends, recvs, 0

    def copy(self, src, dst, device):
        k = self.used
        self.used += 1
        return pltpu.make_async_remote_copy(
            src_ref=src, dst_ref=dst, send_sem=self.sends.at[k], recv_sem=self.recvs.at[k],
            device_id=device, device_id_type=MESH,
        )


def gather_copies(links, nh, s, h, beside, src, out, size, spot):
    far = []
    for k in range(2, nh, 2):
        to = lax.rem(h + k, nh)
        first = links.copy(src, out.at[spot(h)], (s, to))
        came = out.at[spot(lax.rem(h + nh - k, nh))]
        far.append((first, links.copy(came, came, (s, beside))))
    near = links.copy(src, out.at[spot(h)], (s, beside))
    return far, near


def spread_piece(links, nh, s, h, beside, out, half, slot):
    spot = lambda owner: block(owner * 2 + slot, half)
    return gather_copies(links, nh, s, h, beside, out.at[spot(h)], out, half, spot)


def start_gather(gather):
    far, near = gather
    for first, _ in far:
        first.start()
    near.start()


def forward_gather(gather):
    for first, second in gather[0]:
        first.wait_recv()
        second.start()


def finish_gather(gather):
    far, near = gather
    for first, second in far:
        first.wait_send()
        second.wait()
    near.wait()


def padded_column(c):
    a = max(a for a in range(HEAD_DIM) if CANON[a] <= c)
    return STARTS[a] + a % 8 + c - CANON[a]


def windows(features, nh):
    wide = features // nh
    ends = [(padded_column(k * wide), padded_column(k * wide + wide - 1)) for k in range(nh)]
    width = max(-(-(hi + 1) // 128) * 128 - lo // 128 * 128 for lo, hi in ends)
    return [min(lo // 128 * 128, PADDED - width) for lo, _ in ends], width


def window_at(starts, owner, nh):
    at = starts[0]
    for k in range(1, nh):
        at = at + (starts[k] - starts[k - 1]) * ((owner + nh - k) // nh)
    return at


def masked(full, causal):
    n = full.shape[0]
    last = jnp.where(causal, full[n - CHUNK :], 0.0)
    if n == CHUNK:
        return last.astype(BF16)
    return jnp.concatenate([full[: n - CHUNK], last], axis=0).astype(BF16)


def main_kernel(ns, nh, names, starts, width, *refs):
    r = dict(zip(names, refs))
    q_ref, kv_ref, init_ref, og_ref = r["q"], r["kv"], r["init"], r["og"]
    kvt, xs, x, row, df, f_all = r["kvt"], r["xs"], r["x"], r["row"], r["df"], r["f"]
    qt, ogt, attt, qgt, dnt = r["qt"], r["ogt"], r["attt"], r["qgt"], r["dnt"]
    start, startt, keys, vals, kt, vt = (
        r["start"], r["startt"], r["keys"], r["vals"], r["kt"], r["vt"]
    )
    carry, later_ref, sg, kvl = r["carry"], r["later"], r["sg"], r["kvl"]
    padt, tall = r["padt"], r["tall"]
    tokens = q_ref.shape[0]
    heads = q_ref.shape[1] // HEAD_DIM
    chunks = tokens // CHUNK
    features = init_ref.shape[1]
    rows, quarter, half, groups = HEAD_DIM // nh, tokens // nh, HEAD_DIM // nh // 2, ns // 2
    s, h, g, p, beside, partner, ring, across = places(ns, nh)
    links = Links(r["sends"], r["recvs"])
    barrier = pltpu.get_barrier_semaphore()
    for device in [partner] + ring + across:
        pl.semaphore_signal(barrier, inc=1, device_id=device, device_id_type=MESH)

    kvt[...] = kv_ref[...].astype(F32).T
    mine_vals = kvt[block(HEAD_DIM // rows + h, rows), :].astype(BF16)
    u_ref = r["u"]
    for c in range(chunks):
        at = slice(c * CHUNK, (c + 1) * CHUNK)
        xk = kvt.at[:HEAD_DIM, at]
        xs[...] = scaled(xk[...])
        write_features(xk, xs, f_all.at[c], CHUNK)
        part = dot(mine_vals[:, at], f_all[c], ((1,), (1,)))
        if c == 0:
            u_ref[...] = part
        else:
            u_ref[...] += part
    pl.semaphore_wait(barrier, 1 + len(ring) + len(across))
    pair = r["pair"]
    swap = links.copy(u_ref.at[block(1 - p, half), :], pair, partner)
    swap.start()

    qt[...] = q_ref[...].astype(F32).T
    kt[...] = kvt[:HEAD_DIM, :].astype(BF16)
    vt[...] = kvt[HEAD_DIM:, :].astype(BF16)
    keys[...] = kv_ref[:, :HEAD_DIM]
    vals[...] = kv_ref[:, HEAD_DIM:]
    causal = lax.broadcasted_iota(jnp.int32, (CHUNK, CHUNK), 0) <= lax.broadcasted_iota(
        jnp.int32, (CHUNK, CHUNK), 1
    )

    def inner(c):
        n = (c + 1) * CHUNK
        at = slice(c * CHUNK, n)

        def one_head(k, _):
            here = pl.ds(pl.multiple_of(k * HEAD_DIM, HEAD_DIM), HEAD_DIM)
            query = qt[here, at]
            x[...] = query
            xs[...] = scaled(query)
            write_features(x, xs, f_all.at[c * heads + k], CHUNK)
            logits = dot(keys[:n], query.astype(BF16))
            weights = masked(logits * logits * (1.0 / HEAD_DIM), causal)
            r[f"logits{c}"][k] = logits
            r[f"weights{c}"][k] = weights
            attt[here, at] = dot(vt[:, :n], weights)
            return 0

        lax.fori_loop(0, heads, one_head, 0)

    def upward(c):
        n = (c + 1) * CHUNK
        at = slice(c * CHUNK, n)

        def one_head(k, _):
            here = pl.ds(pl.multiple_of(k * HEAD_DIM, HEAD_DIM), HEAD_DIM)
            query = qt[here, at]
            xs[...] = scaled(query)
            dn = dnt[here, at]
            df[...] = dot(startt[...], dn)
            dw = dot(vals[:n], dn)
            dl = masked(dw * r[f"logits{c}"][k] * (2.0 / HEAD_DIM), causal)
            qgt[here, at] = dot(kt[:, :n], dl) + feature_grad(xs, df, row, CHUNK)
            kvl[:n, :HEAD_DIM] += dot(dl, query.astype(BF16), ((1,), (1,)))
            kvl[:n, HEAD_DIM:] += dot(r[f"weights{c}"][k], dn, ((1,), (1,)))
            return 0

        lax.fori_loop(0, heads, one_head, 0)

    swap.wait()
    both = r["both"]
    mine = u_ref[block(p, half), :]
    both[...] = mine + pair[...]
    moves = [links.copy(both, r["got"].at[k], ring[k]) for k in range(groups - 1)]
    for k, move in enumerate(moves):
        @pl.when(g + k + 1 < groups)
        def _(move=move):
            move.start()
    order = list(range(chunks))
    inner(order[-1])
    for c in order[:-3]:
        inner(c)
    ours = block(h * 2 + p, half)
    mate = r["mate"]
    base, mated = jnp.where(p == 1, pair[...], 0.0), jnp.where(p == 0, mine, 0.0)
    carry[ours, :] = base
    mate[...] = mated
    for k, move in enumerate(moves):
        @pl.when(g - k - 1 >= 0)
        def _(move=move, k=k):
            move.wait_recv()
            carry[ours, :] += r["got"][k]
            mate[...] += r["got"][k]
    back = links.copy(mate, carry.at[ours, :], partner)
    back.start()
    own_half = spread_piece(links, nh, s, h, beside, carry, half, p)
    start_gather(own_half)
    inner(order[-3])
    other_half = spread_piece(links, nh, s, h, beside, carry, half, 1 - p)
    back.wait_recv()
    start_gather(other_half)
    forward_gather(own_half)
    inner(order[-2])
    forward_gather(other_half)

    wide = r["wide"]
    whole_lanes = features // 128 * 128
    padt[...] = jnp.zeros_like(padt)
    wide[:, whole_lanes:] = jnp.zeros_like(wide[:, whole_lanes:])
    wide[:, :features] = init_ref[...]
    tall[...] = wide[...].T
    for a in range(HEAD_DIM):
        at = STARTS[a] + a % 8
        padt[at : at + HEAD_DIM - a, :] = tall[CANON[a] : CANON[a] + HEAD_DIM - a, :]
    initp = padt[...].T
    ogt[...] = og_ref[...].astype(F32).T
    for k, move in enumerate(moves):
        @pl.when(g + k + 1 < groups)
        def _(move=move):
            move.wait_send()
    back.wait_send()
    finish_gather(own_half)
    finish_gather(other_half)
    first_state = initp + carry[...]
    start[...] = first_state.astype(BF16)
    startt[...] = first_state.T.astype(BF16)

    sg[...] = jnp.zeros_like(sg)

    def normalize(i, _):
        c, k = i // heads, lax.rem(i, heads)
        here = pl.ds(pl.multiple_of(k * HEAD_DIM, HEAD_DIM), HEAD_DIM)
        at = pl.ds(pl.multiple_of(c * CHUNK, CHUNK), CHUNK)
        numer = attt[here, at] + dot(start[...], f_all[i])
        scale = lax.rsqrt(jnp.mean(numer * numer, axis=0, keepdims=True) + EPS)
        normed = numer * scale
        up = ogt[here, at]
        attt[here, at] = normed
        dn = (scale * (up - normed * jnp.mean(up * normed, axis=0, keepdims=True))).astype(BF16)
        dnt[here, at] = dn
        sg[...] += dot(dn, f_all[i], ((1,), (1,)))
        return 0

    lax.fori_loop(0, chunks * heads, normalize, 0)

    near, far, mid, own = r["near"], r["far"], r["mid"], r["own"]
    evens = range(2, nh + 1, 2)
    first, second = [], []
    for i, k in enumerate(evens):
        src = sg.at[block(lax.rem(beside + k, nh), rows), :]
        first.append(links.copy(src, near.at[i], (s, beside)))
        first[-1].start()
    kvl[...] = jnp.zeros_like(kvl)
    upward(0)
    for i, k in enumerate(evens):
        first[i].wait_recv()
        summed = sg[block(lax.rem(h + k, nh), rows), :] + near[i]
        if k == nh:
            own[...] = summed
        else:
            mid[i] = summed
            second.append(links.copy(mid.at[i], far.at[i], (s, lax.rem(h + k, nh))))
            second[-1].start()
    for c in order[1:-2]:
        upward(c)
    for i, copy in enumerate(second):
        copy.wait_recv()
        own[...] += far[i]
    spair, sboth = r["spair"], r["sboth"]
    sswap = links.copy(own.at[block(1 - p, half), :], spair, partner)
    sswap.start()
    att_ref, qg_ref = r["att"], r["qg"]
    upward(order[-2])
    sswap.wait()
    mine = own[block(p, half), :]
    sboth[...] = mine + spair[...]
    smoves = [links.copy(sboth, r["sgot"].at[k], ring[k]) for k in range(groups - 1)]
    for move in smoves:
        move.start()
    upward(order[-1])
    kvparts, kvscatter = r["kvparts"], []
    for k in range(nh - 1):
        src = kvl.at[block(lax.rem(h + k + 1, nh), quarter), :]
        kvscatter.append(links.copy(src, kvparts.at[k], across[k]))
        kvscatter[-1].start()
    smate, tot, total_ref = r["smate"], r["tot"], r["total"]
    later = jnp.where(p == 0, spair[...], 0.0)
    mated = jnp.where(p == 1, mine, 0.0)
    whole = sboth[...]
    for k, move in enumerate(smoves):
        move.wait_recv()
        whole = whole + r["sgot"][k]
        after = jnp.where(k + 1 > g, r["sgot"][k], 0.0)
        later = later + after
        mated = mated + after
    later_ref[ours, :] = later
    smate[...] = mated
    tot[...] = whole
    sback = links.copy(smate, later_ref.at[ours, :], partner)
    sback.start()
    own_half = spread_piece(links, nh, s, h, beside, later_ref, half, p)
    start_gather(own_half)
    total_swap = links.copy(tot, total_ref.at[block(p, half), :], partner)
    total_swap.start()
    other_half = spread_piece(links, nh, s, h, beside, later_ref, half, 1 - p)
    kq, vq = r["kq"], r["vq"]
    kvq = kv_ref[pl.ds(pl.multiple_of(h * quarter, 16), quarter), :].astype(F32).T
    kq[...] = kvq[:HEAD_DIM]
    vq[...] = kvq[HEAD_DIM:].astype(BF16)
    xs[...] = scaled(kq[...])
    write_features(kq, xs, f_all.at[0], quarter)
    sback.wait_recv()
    start_gather(other_half)
    total_ref[block(p, half), :] = tot[...]
    forward_gather(own_half)
    att_ref[...] = attt[...].T.astype(BF16)
    forward_gather(other_half)
    qg_ref[...] = qgt[...].T.astype(BF16)
    kvsum = kvl[block(h, quarter), :]
    for k, copy in enumerate(kvscatter):
        copy.wait()
        kvsum = kvsum + kvparts[k]
    r["kvsum"][...] = kvsum
    for copy in first + second + smoves + [sback]:
        copy.wait_send()
    total_swap.wait()
    finish_gather(own_half)
    finish_gather(other_half)

    win = r["win"]
    wins = []
    for k in range(nh - 1):
        to = lax.rem(h + k + 1, nh)
        columns = pl.ds(pl.multiple_of(window_at(starts, to, nh), 128), width)
        wins.append(links.copy(total_ref.at[:, columns], win.at[block(h, rows), :], across[k]))
        wins[-1].start()
    own_window = pl.ds(pl.multiple_of(window_at(starts, h, nh), 128), width)
    win[block(h, rows), :] = total_ref[:, own_window]
    later_state = later_ref[...]
    start[...] = later_state.astype(BF16)
    startt[...] = later_state.T.astype(BF16)
    gt = r["gt"]
    gt[HEAD_DIM:, :] = dot(start[...], f_all[0])
    df[...] = dot(startt[...], vq[...])
    gt[:HEAD_DIM, :] = feature_grad(xs, df, row, quarter)
    part_ref, kv_out = r["part"], r["kv_grad"]
    part_ref[...] = r["kvsum"][...] + gt[...].T
    spot = lambda owner: block(owner, quarter)
    parts = gather_copies(links, nh, s, h, beside, part_ref, kv_out, quarter, spot)
    start_gather(parts)
    kv_out[spot(h), :] = part_ref[...]
    for move in wins:
        move.wait()
    padt[own_window, :] = win[...].T
    forward_gather(parts)
    canon = r["tall"]
    for a in range(HEAD_DIM):
        at = STARTS[a] + a % 8
        canon[CANON[a] : CANON[a] + HEAD_DIM - a, :] = padt[at : at + HEAD_DIM - a, :]
    slice_width = features // nh
    flip, init_out = r["flip"], r["init_grad"]
    flip[:slice_width, :] = canon[block(h, slice_width), :]
    init_out[...] = flip[...].T[:, :slice_width]
    finish_gather(parts)


def per_device(ns, nh, queries, keys_values, init_state, out_grad):
    tokens, wide = queries.shape
    assert tokens == GROUP and ns % 2 == 0 and nh % 2 == 0 and tokens // nh == CHUNK
    features = init_state.shape[1]
    heads = wide // HEAD_DIM
    rows, quarter, groups = HEAD_DIM // nh, tokens // nh, ns // 2
    even = -(-features // 128) * 128
    starts, width = windows(features, nh)
    slice_width = features // nh
    D, V = pltpu.SemaphoreType.DMA, pltpu.VMEM
    part, piece, state = (rows, PADDED), (rows // 2, PADDED), (HEAD_DIM, PADDED)
    columns, chunk = (wide, tokens), (HEAD_DIM, CHUNK)
    count = 2 + groups - 1 + 2 * (nh - 1)
    count += nh // 2 + nh // 2 - 1 + nh - 1 + 3 + groups - 1 + 2 * (nh - 1)
    count += nh - 1 + nh - 1
    outs = dict(
        att=((tokens, wide), BF16),
        qg=((tokens, wide), BF16),
        kv_grad=((tokens, 2 * HEAD_DIM), F32),
        init_grad=((HEAD_DIM, slice_width), F32),
    )
    scratch = dict(
        kvt=V((2 * HEAD_DIM, tokens), F32), x=V(chunk, F32), xs=V(chunk, F32), row=V(chunk, F32),
        df=V((PADDED, CHUNK), F32), f=V((tokens // CHUNK * heads, PADDED, CHUNK), BF16),
        qt=V(columns, F32), ogt=V(columns, F32), attt=V(columns, F32), qgt=V(columns, F32),
        dnt=V(columns, BF16), start=V(state, BF16), startt=V((PADDED, HEAD_DIM), BF16),
        keys=V((tokens, HEAD_DIM), BF16), vals=V((tokens, HEAD_DIM), BF16),
        kt=V((HEAD_DIM, tokens), BF16), vt=V((HEAD_DIM, tokens), BF16),
        carry=V(state, F32), later=V(state, F32), sg=V(state, F32),
        kvl=V((tokens, 2 * HEAD_DIM), F32), padt=V((PADDED, HEAD_DIM), F32),
        tall=V((even, HEAD_DIM), F32), wide=V((HEAD_DIM, even), F32),
        u=V(part, F32), pair=V(piece, F32), both=V(piece, F32), mate=V(piece, F32),
        got=V((groups - 1,) + piece, F32),
        near=V((nh // 2,) + part, F32), far=V((nh // 2,) + part, F32),
        mid=V((nh // 2,) + part, F32), own=V(part, F32), spair=V(piece, F32),
        sboth=V(piece, F32), smate=V(piece, F32), tot=V(piece, F32), total=V(part, F32),
        sgot=V((groups - 1,) + piece, F32), kvparts=V((nh - 1, quarter, 2 * HEAD_DIM), F32),
        kq=V((HEAD_DIM, quarter), F32), vq=V((HEAD_DIM, quarter), BF16),
        kvsum=V((quarter, 2 * HEAD_DIM), F32), gt=V((2 * HEAD_DIM, quarter), F32),
        part=V((quarter, 2 * HEAD_DIM), F32), win=V((HEAD_DIM, width), F32),
        flip=V((-(-slice_width // 128) * 128, HEAD_DIM), F32),
        sends=D((count,)), recvs=D((count,)),
    )
    for c in range(tokens // CHUNK):
        scratch[f"logits{c}"] = V((heads, (c + 1) * CHUNK, CHUNK), F32)
        scratch[f"weights{c}"] = V((heads, (c + 1) * CHUNK, CHUNK), BF16)
    names = ["q", "kv", "init", "og"] + list(outs) + list(scratch)
    vmem = pl.BlockSpec(memory_space=pltpu.VMEM)
    return pl.pallas_call(
        functools.partial(main_kernel, ns, nh, names, starts, width),
        out_shape=tuple(jax.ShapeDtypeStruct(*out) for out in outs.values()),
        in_specs=[vmem] * 4,
        out_specs=(vmem,) * len(outs),
        scratch_shapes=list(scratch.values()),
        compiler_params=pltpu.CompilerParams(
            vmem_limit_bytes=62 * 1024 * 1024, collective_id=1, has_side_effects=True
        ),
    )(queries, keys_values, init_state, out_grad)


def solution(mesh):
    ns, nh = mesh.shape["seq"], mesh.shape["head"]
    return jax.shard_map(
        functools.partial(per_device, ns, nh),
        mesh=mesh,
        in_specs=(P("seq", "head"), P("seq", None), P(), P("seq", "head")),
        out_specs=(P("seq", "head"), P("seq", "head"), P("seq", None), P(None, "head")),
        check_vma=False,
    )
```

time: 133 us -> 86.3 us (0.65)
  the two profiles are of different devices: /device:TPU:9 before, /device:TPU:0 now
where the time goes in v3:
time: 86.3 us; the launch traced here: 85.9 us
  Pallas kernels  80.4 us (93%)
  local copies, waits for them, and re-layouts  4.88 us (6%)
    pallas_call x1, Pallas kernels, per_device(): pl.pallas_call(functools.partial(main_kernel, ns, nh, names, starts, widt...  80.4 us
    unnamed x10, local copies, waits for them, and re-layouts  4.88 us

profile of v3, /device:TPU:0, one launch (start us, length us, event | category | flops | bytes accessed | tf_op | source)
XLA Modules:
  0.0 85.9 jit_solution(6283310340014123329)
XLA Ops:
  0.6 80.4 %shard_map.75 = (bf16[1024,256]{1,0:T(8,128)(2,1)}, bf16[1024,256]{1,0:T(8,128)(2,1)}, f32[1024,128]{1,0:T(8,128)}, f32[64,520]{1,0:T(8,128)}) custom-call(bf16[1024,256]{1,0:T(8,128)(2,1)} %refs_0_.1, bf16[1024,128]{1,0:T(8,128)(2,1)} %refs_1_.1, f32[64,2080]{1,0:T(8,128)} %refs_2_.1, bf16[1024,256]{1,0:T(8,128)(2,1)} %refs_3_.1), custom_call_target="tpu_custom_call" | custom-call | tf_op jit(solution)/shard_map/pallas_call | solution.py:504
  81.0 0.0 copy-start.1
  81.0 1.9 %copy.12 = bf16[1024,256]{1,0:T(8,128)(2,1)} copy(bf16[1024,256]{1,0:T(8,128)(2,1)} %get-tuple-element.8) | data formatting | bytes 1048576
  82.9 0.0 copy-done.1
  82.9 0.0 copy-start
  82.9 0.8 copy.13
  83.7 0.4 copy-done
  84.2 0.0 copy-start.2
  84.2 0.8 copy.14
  85.0 0.3 copy-done.2
  85.2 0.7 copy.15
Async XLA Ops:
  81.0 1.9 %copy-start.1 = (bf16[1024,256]{1,0:T(8,128)(2,1)S(1)}, bf16[1024,256]{1,0:T(8,128)(2,1)}, u32[]{:S(2)}) copy-start(bf16[1024,256]{1,0:T(8,128)(2,1)} %get-tuple-element.9) | copy-start | bytes 1572868
  82.9 1.2 %copy-start = (f32[1024,128]{1,0:T(8,128)S(1)}, f32[1024,128]{1,0:T(8,128)}, u32[]{:S(2)}) copy-start(f32[1024,128]{1,0:T(8,128)} %get-tuple-element.10) | copy-start | bytes 1572868
  84.2 1.1 %copy-start.2 = (f32[64,520]{1,0:T(8,128)S(1)}, f32[64,520]{1,0:T(8,128)}, u32[]{:S(2)}) copy-start(f32[64,520]{1,0:T(8,128)} %get-tuple-element.11) | copy-start | bytes 399364

commit v4 on v3

--- a/solution.py
+++ b/solution.py
@@ -256,6 +256,17 @@
 
         lax.fori_loop(0, heads, one_head, 0)
 
+    wide = r["wide"]
+    whole_lanes = features // 128 * 128
+    padt[...] = jnp.zeros_like(padt)
+    wide[:, whole_lanes:] = jnp.zeros_like(wide[:, whole_lanes:])
+    wide[:, :features] = init_ref[...]
+    tall[...] = wide[...].T
+    for a in range(HEAD_DIM):
+        at = STARTS[a] + a % 8
+        padt[at : at + HEAD_DIM - a, :] = tall[CANON[a] : CANON[a] + HEAD_DIM - a, :]
+    r["initp"][...] = padt[...].T
+    ogt[...] = og_ref[...].astype(F32).T
     swap.wait()
     both = r["both"]
     mine = u_ref[block(p, half), :]
@@ -292,17 +303,6 @@
     inner(order[-2])
     forward_gather(other_half)
 
-    wide = r["wide"]
-    whole_lanes = features // 128 * 128
-    padt[...] = jnp.zeros_like(padt)
-    wide[:, whole_lanes:] = jnp.zeros_like(wide[:, whole_lanes:])
-    wide[:, :features] = init_ref[...]
-    tall[...] = wide[...].T
-    for a in range(HEAD_DIM):
-        at = STARTS[a] + a % 8
-        padt[at : at + HEAD_DIM - a, :] = tall[CANON[a] : CANON[a] + HEAD_DIM - a, :]
-    initp = padt[...].T
-    ogt[...] = og_ref[...].astype(F32).T
     for k, move in enumerate(moves):
         @pl.when(g + k + 1 < groups)
         def _(move=move):
@@ -310,7 +310,7 @@
     back.wait_send()
     finish_gather(own_half)
     finish_gather(other_half)
-    first_state = initp + carry[...]
+    first_state = r["initp"][...] + carry[...]
     start[...] = first_state.astype(BF16)
     startt[...] = first_state.T.astype(BF16)
 
@@ -367,11 +367,12 @@
     for move in smoves:
         move.start()
     upward(order[-1])
-    kvparts, kvscatter = r["kvparts"], []
-    for k in range(nh - 1):
-        src = kvl.at[block(lax.rem(h + k + 1, nh), quarter), :]
-        kvscatter.append(links.copy(src, kvparts.at[k], across[k]))
-        kvscatter[-1].start()
+    kvnear, kvfar, kvmid = r["kvnear"], r["kvfar"], r["kvmid"]
+    kvfirst, kvsecond = [], []
+    for i, k in enumerate(evens):
+        src = kvl.at[block(lax.rem(beside + k, nh), quarter), :]
+        kvfirst.append(links.copy(src, kvnear.at[i], (s, beside)))
+        kvfirst[-1].start()
     smate, tot, total_ref = r["smate"], r["tot"], r["total"]
     later = jnp.where(p == 0, spair[...], 0.0)
     mated = jnp.where(p == 1, mine, 0.0)
@@ -400,17 +401,22 @@
     write_features(kq, xs, f_all.at[0], quarter)
     sback.wait_recv()
     start_gather(other_half)
+    for i, k in enumerate(evens):
+        kvfirst[i].wait_recv()
+        summed = kvl[block(lax.rem(h + k, nh), quarter), :] + kvnear[i]
+        if k == nh:
+            r["kvsum"][...] = summed
+        else:
+            kvmid[i] = summed
+            to = (s, lax.rem(h + k, nh))
+            kvsecond.append(links.copy(kvmid.at[i], kvfar.at[i], to))
+            kvsecond[-1].start()
     total_ref[block(p, half), :] = tot[...]
     forward_gather(own_half)
     att_ref[...] = attt[...].T.astype(BF16)
     forward_gather(other_half)
     qg_ref[...] = qgt[...].T.astype(BF16)
-    kvsum = kvl[block(h, quarter), :]
-    for k, copy in enumerate(kvscatter):
-        copy.wait()
-        kvsum = kvsum + kvparts[k]
-    r["kvsum"][...] = kvsum
-    for copy in first + second + smoves + [sback]:
+    for copy in first + second + smoves + kvfirst + [sback]:
         copy.wait_send()
     total_swap.wait()
     finish_gather(own_half)
@@ -428,20 +434,26 @@
     later_state = later_ref[...]
     start[...] = later_state.astype(BF16)
     startt[...] = later_state.T.astype(BF16)
-    gt = r["gt"]
-    gt[HEAD_DIM:, :] = dot(start[...], f_all[0])
-    df[...] = dot(startt[...], vq[...])
-    gt[:HEAD_DIM, :] = feature_grad(xs, df, row, quarter)
-    part_ref, kv_out = r["part"], r["kv_grad"]
-    part_ref[...] = r["kvsum"][...] + gt[...].T
-    spot = lambda owner: block(owner, quarter)
-    parts = gather_copies(links, nh, s, h, beside, part_ref, kv_out, quarter, spot)
-    start_gather(parts)
-    kv_out[spot(h), :] = part_ref[...]
+    for i, copy in enumerate(kvsecond):
+        copy.wait()
+        r["kvsum"][...] += kvfar[i]
+    gt, part_ref, kv_out = r["gt"], r["part"], r["kv_grad"]
+    size = quarter // 2
+    gathers = []
+    for j in range(2):
+        at = slice(j * size, (j + 1) * size)
+        gt[HEAD_DIM:, at] = dot(start[...], f_all[0, :, at])
+        df[:, at] = dot(startt[...], vq[:, at])
+        gt[:HEAD_DIM, at] = feature_grad(xs.at[:, at], df.at[:, at], row.at[:, at], size)
+        part_ref[at, :] = r["kvsum"][at, :] + gt[:, at].T
+        spot = lambda owner, j=j: block(owner * 2 + j, size)
+        gathers.append(gather_copies(links, nh, s, h, beside, part_ref.at[at, :], kv_out, size, spot))
+        start_gather(gathers[-1])
     for move in wins:
         move.wait()
     padt[own_window, :] = win[...].T
-    forward_gather(parts)
+    kv_out[block(h, quarter), :] = part_ref[...]
+    forward_gather(gathers[0])
     canon = r["tall"]
     for a in range(HEAD_DIM):
         at = STARTS[a] + a % 8
@@ -449,8 +461,30 @@
     slice_width = features // nh
     flip, init_out = r["flip"], r["init_grad"]
     flip[:slice_width, :] = canon[block(h, slice_width), :]
+    forward_gather(gathers[1])
     init_out[...] = flip[...].T[:, :slice_width]
-    finish_gather(parts)
+    for gather in gathers:
+        finish_gather(gather)
+
+
+def deliver_kernel(count, *refs):
+    sems = refs[-1]
+    copies = [pltpu.make_async_copy(refs[i], refs[count + i], sems.at[i]) for i in range(count)]
+    for copy in copies:
+        copy.start()
+    for copy in copies:
+        copy.wait()
+
+
+def deliver(arrays):
+    hbm = pl.BlockSpec(memory_space=pl.ANY)
+    return pl.pallas_call(
+        functools.partial(deliver_kernel, len(arrays)),
+        out_shape=tuple(jax.ShapeDtypeStruct(x.shape, x.dtype) for x in arrays),
+        in_specs=[hbm] * len(arrays),
+        out_specs=(hbm,) * len(arrays),
+        scratch_shapes=[pltpu.SemaphoreType.DMA((len(arrays),))],
+    )(*arrays)
 
 
 def per_device(ns, nh, queries, keys_values, init_state, out_grad):
@@ -466,8 +500,8 @@
     part, piece, state = (rows, PADDED), (rows // 2, PADDED), (HEAD_DIM, PADDED)
     columns, chunk = (wide, tokens), (HEAD_DIM, CHUNK)
     count = 2 + groups - 1 + 2 * (nh - 1)
-    count += nh // 2 + nh // 2 - 1 + nh - 1 + 3 + groups - 1 + 2 * (nh - 1)
-    count += nh - 1 + nh - 1
+    count += 2 * (nh - 1) + 3 + groups - 1 + 2 * (nh - 1)
+    count += 3 * (nh - 1)
     outs = dict(
         att=((tokens, wide), BF16),
         qg=((tokens, wide), BF16),
@@ -489,7 +523,10 @@
         near=V((nh // 2,) + part, F32), far=V((nh // 2,) + part, F32),
         mid=V((nh // 2,) + part, F32), own=V(part, F32), spair=V(piece, F32),
         sboth=V(piece, F32), smate=V(piece, F32), tot=V(piece, F32), total=V(part, F32),
-        sgot=V((groups - 1,) + piece, F32), kvparts=V((nh - 1, quarter, 2 * HEAD_DIM), F32),
+        sgot=V((groups - 1,) + piece, F32), kvnear=V((nh // 2, quarter, 2 * HEAD_DIM), F32),
+        kvfar=V((nh // 2, quarter, 2 * HEAD_DIM), F32),
+        kvmid=V((nh // 2, quarter, 2 * HEAD_DIM), F32),
+        initp=V(state, F32),
         kq=V((HEAD_DIM, quarter), F32), vq=V((HEAD_DIM, quarter), BF16),
         kvsum=V((quarter, 2 * HEAD_DIM), F32), gt=V((2 * HEAD_DIM, quarter), F32),
         part=V((quarter, 2 * HEAD_DIM), F32), win=V((HEAD_DIM, width), F32),
@@ -501,7 +538,7 @@
         scratch[f"weights{c}"] = V((heads, (c + 1) * CHUNK, CHUNK), BF16)
     names = ["q", "kv", "init", "og"] + list(outs) + list(scratch)
     vmem = pl.BlockSpec(memory_space=pltpu.VMEM)
-    return pl.pallas_call(
+    results = pl.pallas_call(
         functools.partial(main_kernel, ns, nh, names, starts, width),
         out_shape=tuple(jax.ShapeDtypeStruct(*out) for out in outs.values()),
         in_specs=[vmem] * 4,
@@ -511,6 +548,7 @@
             vmem_limit_bytes=62 * 1024 * 1024, collective_id=1, has_side_effects=True
         ),
     )(queries, keys_values, init_state, out_grad)
+    return deliver(results)
 
 
 def solution(mesh):

time: 86.3 us -> 135 us (1.56)
  Pallas kernels: 80.4 us -> 134 us
  local copies, waits for them, and re-layouts: 4.88 us -> 0 us
    pallas_call x0 -> x1, Pallas kernels: none -> 53.7 us  [deliver(): pl.pallas_call(functools.partial(deliver_kernel, len(arrays)), out_shape=...]
    unnamed x10 -> x0, local copies, waits for them, and re-layouts: 4.88 us -> none
where the time goes in v4:
time: 135 us
  Pallas kernels  134 us (99%)
    pallas_call x1, Pallas kernels, per_device(): pl.pallas_call(functools.partial(main_kernel, ns, nh, names, starts, widt...  80.4 us
    pallas_call x1, Pallas kernels, deliver(): pl.pallas_call(functools.partial(deliver_kernel, len(arrays)), out_shape=...  53.7 us

profile of v4, /device:TPU:0, one launch (start us, length us, event | category | flops | bytes accessed | tf_op | source)
XLA Modules:
  0.0 134.7 jit_solution(8331491474827696909)
XLA Ops:
  0.6 80.4 %shard_map.75 = (bf16[1024,256]{1,0:T(8,128)(2,1)}, bf16[1024,256]{1,0:T(8,128)(2,1)}, f32[1024,128]{1,0:T(8,128)}, f32[64,520]{1,0:T(8,128)}) custom-call(bf16[1024,256]{1,0:T(8,128)(2,1)} %refs_0_.1, bf16[1024,128]{1,0:T(8,128)(2,1)} %refs_1_.1, f32[64,2080]{1,0:T(8,128)} %refs_2_.1, bf16[1024,256]{1,0:T(8,128)(2,1)} %refs_3_.1), custom_call_target="tpu_custom_call" | custom-call | tf_op jit(solution)/shard_map/pallas_call | solution.py:541
  81.0 53.7 %shard_map.76 = (bf16[1024,256]{1,0:T(8,128)(2,1)}, bf16[1024,256]{1,0:T(8,128)(2,1)}, f32[1024,128]{1,0:T(8,128)}, f32[64,520]{1,0:T(8,128)}) custom-call(bf16[1024,256]{1,0:T(8,128)(2,1)} %get-tuple-element.8.refs_0_, bf16[1024,256]{1,0:T(8,128)(2,1)} %get-tuple-element.9.refs_1_, f32[1024,128]{1,0:T(8,128)} %get-tuple-element.10.refs_2_, ...), custom_call_target="tpu_custom_call" | custom-call | tf_op jit(solution)/shard_map/pallas_call | solution.py:481
